TPU v7x, 32 devices: a whole 2x2x4 slice. The times are simulated.
32 devices in a mesh: section: 2 (over core), dp: 16 (over z, y, x).
Axes of the slice: x: 2, y: 2, z: 4, core: 2. Of those that a mesh axis runs over, the one named last changes fastest.
Arguments:
- tokens: bfloat16 [32768, 768], P('dp'), may hold values from -6 to 6
- out_grad: bfloat16 [32768, 768], P('dp'), may hold values from -6 to 6
- seq_lengths: int32 [32, 8], P('dp'), may hold values from 0 to 1024, as said below
- half_weights: bfloat16 [2, 768, 3072], P('section', 'dp'), may hold values from -0.21875 to 0.21875
- down_weight: bfloat16 [3072, 768], P(('section', 'dp')), may hold values from -0.109375 to 0.109375
- pre_gain: float32 [768], replicated, may hold values from 0.25 to 1.75
- pre_shift: float32 [768], replicated, may hold values from -2 to 2
- query_bias: float32 [768], replicated, may hold values from -2 to 2
- value_bias: float32 [768], replicated, may hold values from -2 to 2
- sub_gain: float32 [768], replicated, may hold values from 0.25 to 1.75
- sub_shift: float32 [768], replicated, may hold values from -2 to 2
- out_bias: float32 [768], replicated, may hold values from -2 to 2
- ffn_gain: float32 [768], replicated, may hold values from 0.25 to 1.75
- ffn_shift: float32 [768], replicated, may hold values from -2 to 2
- up_bias: float32 [3072], replicated, may hold values from -2 to 2
- mid_gain: float32 [3072], replicated, may hold values from 0.25 to 1.75
- mid_shift: float32 [3072], replicated, may hold values from -2 to 2
- down_bias: float32 [768], replicated, may hold values from -2 to 2
Outputs:
- layer_out: float32 [32768, 768], P('dp')
- tokens_grad: float32 [32768, 768], P('dp', 'section')
- half_weights_grad: float32 [2, 768, 3072], P('section', 'dp')
- down_weight_grad: float32 [3072, 768], P(('section', 'dp'))
- pre_gain_grad: float32 [768], P(('section', 'dp'))
- pre_shift_grad: float32 [768], P(('section', 'dp'))
- query_bias_grad: float32 [768], P(('section', 'dp'))
- value_bias_grad: float32 [768], P(('section', 'dp'))
- sub_gain_grad: float32 [768], P(('section', 'dp'))
- sub_shift_grad: float32 [768], P(('section', 'dp'))
- out_bias_grad: float32 [768], P(('section', 'dp'))
- ffn_gain_grad: float32 [768], P(('section', 'dp'))
- ffn_shift_grad: float32 [768], P(('section', 'dp'))
- up_bias_grad: float32 [3072], P(('section', 'dp'))
- mid_gain_grad: float32 [3072], P(('section', 'dp'))
- mid_shift_grad: float32 [3072], P(('section', 'dp'))
- down_bias_grad: float32 [768], P(('section', 'dp'))
Inputs may be any that keep to these rules, and one draw needn't show every extreme that they name: `seq_lengths`: row b lists the lengths of the sequences packed one after another from the first row of micro-batch b; they sum to at most 1024, and the rows after them are padding. Zero marks an unused slot. Some micro-batch holds a single sequence of 1024 rows.
All inputs are finite; a program needn't handle non-finite values.
Results may differ from a plain program's by a relative error of at most 0.013.
Values may be sent and summed in bfloat16 or wider, within the bound.
A program may use at most 136 MiB of HBM per device.

v0:
```python
import jax
import jax.numpy as jnp
from jax import lax
from jax.sharding import PartitionSpec as P

HEAD_DIM = 64


EPS = 1e-05


def passed_along(value, axis, steps):
    count = lax.axis_size(axis)
    first, last = (max(0, -steps), min(count, count - steps))
    return lax.ppermute(value, axis, [(source, source + steps) for source in range(first, last)])


def layer_norm(value, gain, shift):
    center = jnp.mean(value, axis=-1, keepdims=True)
    centered = value - center
    spread = jnp.mean(centered * centered, axis=-1, keepdims=True)
    return centered * lax.rsqrt(spread + EPS) * gain + shift


def exact_gelu(value):
    return jax.nn.gelu(value, approximate=False)


def row_masks(lengths_row, count):
    ends = jnp.cumsum(lengths_row)
    index = jnp.arange(count, dtype=jnp.int32)
    segment = jnp.sum((index[:, None] >= ends[None, :]).astype(jnp.int32), axis=1)
    alive = segment < lengths_row.shape[0]
    same = segment[:, None] == segment[None, :]
    causal = index[None, :] <= index[:, None]
    allowed = same & causal & (alive[:, None] | (index[:, None] == index[None, :]))
    return (alive.astype(jnp.float32), allowed)


def split_groups(block, groups):
    return block.reshape(block.shape[0], groups, -1).transpose(1, 0, 2)


def join_groups(block):
    return block.transpose(1, 0, 2).reshape(block.shape[1], -1)


def per_head(block):
    return block.reshape(block.shape[0], -1, HEAD_DIM)


def masked_scores(query, key, allowed):
    scores = jnp.einsum(
        "qhd,khd->hqk", per_head(query), per_head(key), preferred_element_type=jnp.float32
    )
    return jnp.where(allowed[None], scores * HEAD_DIM ** (-0.5), -1e30)


def contract_rows(left, right):
    return lax.dot_general(
        left, right, (((0,), (0,)), ((), ())), preferred_element_type=jnp.float32
    )


def contract_cols(left, right):
    return lax.dot_general(
        left, right, (((1,), (1,)), ((), ())), preferred_element_type=jnp.float32
    )


def attention_forward(x_block, alive, allowed, weights, vectors):
    pre_gain, pre_shift, query_bias, value_bias, sub_gain, sub_shift, out_bias = vectors
    count, width = x_block.shape
    groups = width // (4 * HEAD_DIM)
    inputs = x_block.astype(jnp.float32)
    normed = layer_norm(inputs, pre_gain, pre_shift).astype(jnp.bfloat16)
    biases = jnp.concatenate([query_bias, jnp.zeros_like(query_bias), value_bias])
    projected = (
        jnp.dot(normed, weights[:, : 3 * width], preferred_element_type=jnp.float32) + biases
    ).astype(jnp.bfloat16)
    query = split_groups(projected[:, :width], groups)
    key = split_groups(projected[:, width : 2 * width], groups)
    value = split_groups(projected[:, 2 * width :], groups)

    def one_group(parts):
        query_g, key_g, value_g = parts
        scores = masked_scores(query_g, key_g, allowed)
        peak = jnp.max(scores, axis=-1, keepdims=True)
        raised = jnp.exp(scores - peak)
        denominator = jnp.sum(raised, axis=-1, keepdims=True)
        attention = (raised / denominator).astype(jnp.bfloat16)
        context = jnp.einsum(
            "hqk,khd->qhd", attention, per_head(value_g), preferred_element_type=jnp.float32
        )
        return (context.reshape(count, -1), (peak + jnp.log(denominator))[..., 0])

    context, logsum = lax.map(one_group, (query, key, value))
    context = join_groups(context)
    mixed = layer_norm(context, sub_gain, sub_shift).astype(jnp.bfloat16)
    branch = jnp.dot(mixed, weights[:, 3 * width :], preferred_element_type=jnp.float32) + out_bias
    hidden = (inputs + alive[:, None] * branch).astype(jnp.bfloat16)
    return (hidden, projected, logsum, context)


def attention_backward(
    x_block, alive, allowed, weights, vectors, projected, logsum, context, grad_hidden
):
    pre_gain, pre_shift, query_bias, value_bias, sub_gain, sub_shift, out_bias = vectors
    count, width = x_block.shape
    groups = width // (4 * HEAD_DIM)
    upstream = grad_hidden.astype(jnp.float32)
    grad_branch = (alive[:, None] * upstream).astype(jnp.bfloat16)
    mixed, mixed_back = jax.vjp(layer_norm, context, sub_gain, sub_shift)
    mixed = mixed.astype(jnp.bfloat16)
    out_weight = weights[:, 3 * width :]
    grad_out_weight = contract_rows(mixed, grad_branch)
    grad_out_bias = jnp.sum(grad_branch.astype(jnp.float32), axis=0)
    grad_mixed = contract_cols(grad_branch, out_weight)
    grad_context, grad_sub_gain, grad_sub_shift = mixed_back(grad_mixed)
    grad_context = split_groups(grad_context.astype(jnp.bfloat16), groups)
    query = split_groups(projected[:, :width], groups)
    key = split_groups(projected[:, width : 2 * width], groups)
    value = split_groups(projected[:, 2 * width :], groups)

    def one_group(parts):
        query_g, key_g, value_g, grad_g, logsum_g = parts
        scores = masked_scores(query_g, key_g, allowed)
        soft = jnp.exp(scores - logsum_g[..., None])
        grad_heads = per_head(grad_g)
        grad_soft = jnp.einsum(
            "qhd,khd->hqk", grad_heads, per_head(value_g), preferred_element_type=jnp.float32
        )
        grad_value = jnp.einsum(
            "hqk,qhd->khd",
            soft.astype(jnp.bfloat16),
            grad_heads,
            preferred_element_type=jnp.float32,
        )
        inner = jnp.sum(soft * grad_soft, axis=-1, keepdims=True)
        grad_scores = (soft * (grad_soft - inner)).astype(jnp.bfloat16)
        scale = HEAD_DIM ** (-0.5)
        grad_query = (
            jnp.einsum(
                "hqk,khd->qhd", grad_scores, per_head(key_g), preferred_element_type=jnp.float32
            )
            * scale
        )
        grad_key = (
            jnp.einsum(
                "hqk,qhd->khd", grad_scores, per_head(query_g), preferred_element_type=jnp.float32
            )
            * scale
        )
        return (
            grad_query.reshape(count, -1),
            grad_key.reshape(count, -1),
            grad_value.reshape(count, -1),
        )

    grad_query, grad_key, grad_value = lax.map(one_group, (query, key, value, grad_context, logsum))
    grad_projected = jnp.concatenate(
        [join_groups(grad_query), join_groups(grad_key), join_groups(grad_value)], axis=1
    ).astype(jnp.bfloat16)
    inputs = x_block.astype(jnp.float32)
    normed, normed_back = jax.vjp(layer_norm, inputs, pre_gain, pre_shift)
    normed = normed.astype(jnp.bfloat16)
    grad_qkv_weight = contract_rows(normed, grad_projected)
    column_sums = jnp.sum(grad_projected.astype(jnp.float32), axis=0)
    grad_normed = contract_cols(grad_projected, weights[:, : 3 * width])
    grad_inputs, grad_pre_gain, grad_pre_shift = normed_back(grad_normed)
    grad_block = jnp.concatenate([grad_qkv_weight, grad_out_weight], axis=1)
    small = (
        grad_pre_gain,
        grad_pre_shift,
        column_sums[:width],
        column_sums[2 * width :],
        grad_sub_gain,
        grad_sub_shift,
        grad_out_bias,
    )
    return (upstream + grad_inputs, grad_block, small)


def feed_forward(arrived, dy_block, alive, up_weight, down_full, vectors):
    ffn_gain, ffn_shift, up_bias, mid_gain, mid_shift, down_bias = vectors
    hidden = arrived.astype(jnp.float32)
    normed, normed_back = jax.vjp(layer_norm, hidden, ffn_gain, ffn_shift)
    normed = normed.astype(jnp.bfloat16)
    upper = jnp.dot(normed, up_weight, preferred_element_type=jnp.float32) + up_bias
    active, active_back = jax.vjp(exact_gelu, upper)
    middle, middle_back = jax.vjp(layer_norm, active, mid_gain, mid_shift)
    middle = middle.astype(jnp.bfloat16)
    result = (jnp.dot(middle, down_full, preferred_element_type=jnp.float32) + down_bias).astype(
        jnp.bfloat16
    )
    upstream = dy_block.astype(jnp.float32)
    grad_result = (alive[:, None] * upstream).astype(jnp.bfloat16)
    grad_down = contract_rows(middle, grad_result)
    grad_down_bias = jnp.sum(grad_result.astype(jnp.float32), axis=0)
    grad_middle = contract_cols(grad_result, down_full)
    grad_active, grad_mid_gain, grad_mid_shift = middle_back(grad_middle)
    grad_upper = active_back(grad_active)[0].astype(jnp.bfloat16)
    grad_up = contract_rows(normed, grad_upper)
    grad_up_bias = jnp.sum(grad_upper.astype(jnp.float32), axis=0)
    grad_normed = contract_cols(grad_upper, up_weight)
    grad_inputs, grad_ffn_gain, grad_ffn_shift = normed_back(grad_normed)
    grad_back = (upstream + grad_inputs).astype(jnp.bfloat16)
    small = (
        grad_ffn_gain,
        grad_ffn_shift,
        grad_up_bias,
        grad_mid_gain,
        grad_mid_shift,
        grad_down_bias,
    )
    return (jnp.stack([result, grad_back]), grad_up, grad_down, small)


def shards(
    tokens,
    out_grad,
    seq_lengths,
    half_weights,
    down_weight,
    pre_gain,
    pre_shift,
    query_bias,
    value_bias,
    sub_gain,
    sub_shift,
    out_bias,
    ffn_gain,
    ffn_shift,
    up_bias,
    mid_gain,
    mid_shift,
    down_bias,
):
    first = lax.axis_index("section") == 0
    width = tokens.shape[1]
    batches = seq_lengths.shape[0]
    count = tokens.shape[0] // batches
    hidden_units = half_weights.shape[2]
    groups = width // (4 * HEAD_DIM)
    shares = lax.axis_size("section") * lax.axis_size("dp")
    attention_vectors = (pre_gain, pre_shift, query_bias, value_bias, sub_gain, sub_shift, out_bias)
    ffn_vectors = (ffn_gain, ffn_shift, up_bias, mid_gain, mid_shift, down_bias)
    all_vectors = attention_vectors + ffn_vectors

    def fetch():
        block = lax.all_gather(half_weights, "dp", axis=1, tiled=True)[0]
        down_full = lax.all_gather(down_weight, ("section", "dp"), axis=0, tiled=True)
        return (block, down_full)

    def spread(grad_block, grad_down, vectors):
        block_part = lax.psum_scatter(grad_block, "dp", scatter_dimension=0, tiled=True)
        parts = (
            lax.psum_scatter(grad_down, ("section", "dp"), scatter_dimension=0, tiled=True),
            lax.psum_scatter(vectors[0], ("section", "dp"), scatter_dimension=0, tiled=True),
            lax.psum_scatter(vectors[1], ("section", "dp"), scatter_dimension=0, tiled=True),
            lax.psum_scatter(vectors[2], ("section", "dp"), scatter_dimension=0, tiled=True),
            lax.psum_scatter(vectors[3], ("section", "dp"), scatter_dimension=0, tiled=True),
            lax.psum_scatter(vectors[4], ("section", "dp"), scatter_dimension=0, tiled=True),
            lax.psum_scatter(vectors[5], ("section", "dp"), scatter_dimension=0, tiled=True),
            lax.psum_scatter(vectors[6], ("section", "dp"), scatter_dimension=0, tiled=True),
            lax.psum_scatter(vectors[7], ("section", "dp"), scatter_dimension=0, tiled=True),
            lax.psum_scatter(vectors[8], ("section", "dp"), scatter_dimension=0, tiled=True),
            lax.psum_scatter(vectors[9], ("section", "dp"), scatter_dimension=0, tiled=True),
            lax.psum_scatter(vectors[10], ("section", "dp"), scatter_dimension=0, tiled=True),
            lax.psum_scatter(vectors[11], ("section", "dp"), scatter_dimension=0, tiled=True),
            lax.psum_scatter(vectors[12], ("section", "dp"), scatter_dimension=0, tiled=True),
        )
        return (block_part, parts[0], tuple(parts[1:]))

    initial = (
        jnp.zeros((half_weights.shape[1], hidden_units), jnp.float32),
        jnp.zeros(down_weight.shape, jnp.float32),
        tuple((jnp.zeros((vector.shape[0] // shares,), jnp.float32) for vector in all_vectors)),
    )

    def spare_forward():
        return (
            jnp.zeros((count, width), jnp.bfloat16),
            jnp.zeros((count, 3 * width), jnp.bfloat16),
            jnp.zeros((groups, 4, count), jnp.float32),
            jnp.zeros((count, width), jnp.float32),
        )

    def spare_ffn():
        return (
            jnp.zeros((2, count, width), jnp.bfloat16),
            jnp.zeros((width, hidden_units), jnp.float32),
            jnp.zeros((hidden_units, width), jnp.float32),
            tuple((jnp.zeros(vector.shape, jnp.float32) for vector in ffn_vectors)),
        )

    def spare_backward():
        return (
            jnp.zeros((count, width), jnp.float32),
            jnp.zeros((width, hidden_units), jnp.float32),
            tuple((jnp.zeros(vector.shape, jnp.float32) for vector in attention_vectors)),
        )

    def step(carry, inputs):
        x_block, dy_block, lengths_row = inputs
        block, down_full = fetch()
        alive, allowed = row_masks(lengths_row, count)
        hidden, projected, logsum, context = lax.cond(
            first,
            lambda: attention_forward(x_block, alive, allowed, block, attention_vectors),
            spare_forward,
        )
        arrived = passed_along(hidden, "section", 1)
        stacked, grad_up, grad_down, ffn_small = lax.cond(
            first,
            spare_ffn,
            lambda: feed_forward(arrived, dy_block, alive, block, down_full, ffn_vectors),
        )
        returned = passed_along(stacked, "section", -1)
        residual = jnp.where(first, hidden, arrived).astype(jnp.float32)
        branch = jnp.where(first, returned[0], stacked[0]).astype(jnp.float32)
        out_block = residual + alive[:, None] * branch
        grad_x, grad_attention, attention_small = lax.cond(
            first,
            lambda: attention_backward(
                x_block,
                alive,
                allowed,
                block,
                attention_vectors,
                projected,
                logsum,
                context,
                returned[1],
            ),
            spare_backward,
        )
        grad_block = jnp.where(first, grad_attention, grad_up)
        vectors = attention_small + ffn_small
        block_part, down_part, vector_parts = spread(grad_block, grad_down, vectors)
        carry = jax.tree.map(
            lambda total, extra: total + extra, carry, (block_part, down_part, vector_parts)
        )
        return (carry, (out_block, grad_x))

    shaped = (
        tokens.reshape(batches, count, width),
        out_grad.reshape(batches, count, width),
        seq_lengths,
    )
    carry, (outputs, grads) = lax.scan(step, initial, shaped)
    block_part, down_part, vector_parts = carry
    grad_rows = grads.reshape(-1, width)
    half_width = width // 2
    partner_rows = passed_along(
        grad_rows[:, half_width:].astype(jnp.bfloat16), "section", 1
    ).astype(jnp.float32)
    tokens_grad = jnp.where(first, grad_rows[:, :half_width], partner_rows)
    return (
        outputs.reshape(-1, width),
        tokens_grad,
        block_part[None],
        down_part,
        vector_parts[0],
        vector_parts[1],
        vector_parts[2],
        vector_parts[3],
        vector_parts[4],
        vector_parts[5],
        vector_parts[6],
        vector_parts[7],
        vector_parts[8],
        vector_parts[9],
        vector_parts[10],
        vector_parts[11],
        vector_parts[12],
    )


def solution(mesh):
    placed = (
        P("dp", None),
        P("dp", None),
        P("dp", None),
        P("section", "dp", None),
        P(("section", "dp"), None),
        P(),
        P(),
        P(),
        P(),
        P(),
        P(),
        P(),
        P(),
        P(),
        P(),
        P(),
        P(),
        P(),
    )
    return jax.shard_map(
        shards,
        mesh=mesh,
        in_specs=placed,
        out_specs=(
            P("dp", None),
            P("dp", "section"),
            P("section", "dp", None),
            P(("section", "dp"), None),
            P(("section", "dp")),
            P(("section", "dp")),
            P(("section", "dp")),
            P(("section", "dp")),
            P(("section", "dp")),
            P(("section", "dp")),
            P(("section", "dp")),
            P(("section", "dp")),
            P(("section", "dp")),
            P(("section", "dp")),
            P(("section", "dp")),
            P(("section", "dp")),
            P(("section", "dp")),
        ),
        check_vma=False,
    )
```

profile of v0, /device:TPU:0, one launch (start us, length us, event | category | flops | bytes accessed | tf_op | source)
XLA Modules:
  0.0 1942.4 jit_solution(9704926397672733047)
XLA Ops:
  7.4 1917.7 %while.69 = (s32[]{:T(128)}, f32[48,3072]{1,0:T(8,128)}, f32[96,768]{1,0:T(8,128)}, f32[24]{0:T(128)}, f32[24]{0:T(128)}, /*index=5*/f32[24]{0:T(128)}, f32[24]{...) while((s32[]{:T(128)}, f32[48,3072]{1,0:T(8,128)}, ...), condition=%wide.region_63.64_spmd.clone, body=%wide.region_0.63_spmd.clone.sunk | while | flops 47877681152 | bytes 1107301888 | solution.py:351
  15.0 79.5 %all-gather.3.cloned.1.call-done = bf16[1,768,3072]{2,1,0:T(8,128)(2,1)} async-done(((bf16[1,48,3072]{2,1,0:T(8,128)(2,1)}), bf16[1,768,3072]{2,1,0:T(8,128)(2,1)}) %all-gather.3.cloned.1.call-update) | async-done | bytes 4718608 | tf_op jit(solution)/shard_map/while/body/eval_jaxpr/all_gather | solution.py:251
  94.6 78.0 %conditional.9 = (bf16[1024,768]{1,0:T(8,128)(2,1)}, bf16[1024,2304]{1,0:T(8,128)(2,1)}, f32[3,4,1024]{2,1,0:T(4,128)}, f32[1024,768]{0,1:T(8,128)}) conditional(s32[]{:T(128)} %convert_element_type.274, () %tuple.157, (bf16[1024,768]{1,0:T(8,128)(2,1)S(1)}, f32[1024]{0:T(1024)}, f32[768]{0:T(1024)S(1)}, f32[768]{0:T(1024)S(1)}, ...), branch_computations={%region_3.3_spmd, %region_4.12_spmd} | conditional | flops 5981080064 | bytes 124040616 | solution.py:308
  115.2 47.6 %while.67 = (s32[]{:T(128)}, f32[3,1024,256]{1,2,0:T(8,128)}, f32[3,4,1024]{2,1,0:T(4,128)}, bf16[3,1024,256]{1,2,0:T(8,128)(2,1)}, pred[1024,1024]{0,1:T(8,128)...) while((s32[]{:T(128)}, f32[3,1024,256]{1,2,0:T(8,128)}, ...), condition=%wide.region_10.9_spmd, body=%wide.region_7.8_spmd.sunk | while | flops 1124069376 | bytes 61472876 | solution.py:97
  187.4 125.1 %collective-permute-done.1 = bf16[2,1024,768]{2,1,0:T(8,128)(2,1)} collective-permute-done((bf16[2,1024,768]{2,1,0:T(8,128)(2,1)S(1)}, bf16[2,1024,768]{2,1,0:T(8,128)(2,1)}, u32[]{:S(2)}, u32[]{:S(2)}) %collective-permute-start.1) | collective-permute-done | bytes 3145760 | tf_op jit(solution)/shard_map/while/body/eval_jaxpr/ppermute | solution.py:15
  312.7 202.0 %conditional.11 = (f32[768,3072]{1,0:T(8,128)}, f32[768]{0:T(1024)}, f32[768]{0:T(1024)}, f32[768]{0:T(1024)}, f32[768]{0:T(1024)}, /*index=5*/f32[768]{0:T(1024...) conditional(s32[]{:T(128)} %convert_element_type.274, () %tuple.156, (bf16[1024,768]{1,0:T(8,128)(2,1)S(1)}, ...), branch_computations={%region_29.29_spmd, %region_30.47_spmd} | conditional | flops 12495356928 | bytes 345922368 | solution.py:323
  345.0 136.8 %while.68 = (s32[]{:T(128)}, bf16[3,1024,256]{1,2,0:T(8,128)(2,1)}, bf16[3,1024,256]{1,2,0:T(8,128)(2,1)}, bf16[3,1024,256]{1,2,0:T(8,128)(2,1)}, bf16[3,1024,25...) while((s32[]{:T(128)}, bf16[3,1024,256]{1,2,0:T(8,128)(2,1)}, ...), condition=%wide.region_39.38_spmd, body=%wide.region_37.37_spmd.sunk | while | flops 2723147776 | bytes 191971664 | solution.py:160
  353.8 11.3 multiply_reduce_fusion.8
  399.4 11.3 multiply_reduce_fusion.8
  445.0 11.3 multiply_reduce_fusion.8
  533.6 109.7 %all-reduce.18.cloned.1.call-done = (f32[768]{0:T(1024)}, f32[768]{0:T(1024)}, f32[768]{0:T(1024)}, f32[768]{0:T(1024)}, f32[768]{0:T(1024)}, /*index=5*/f32[768...) async-done(((f32[768]{0:T(1024)}, f32[768]{0:T(1024)}, f32[768]{0:T(1024)}, ...) | async-done | bytes 67600 | tf_op jit(solution)/shard_map/while
  648.9 141.1 %reduce-scatter.5.cloned.1.call-done = f32[96,768]{1,0:T(8,128)} async-done(((f32[3072,768]{1,0:T(8,128)}), f32[96,768]{1,0:T(8,128)}) %reduce-scatter.5.cloned.1.call-update) | async-done | bytes 294928 | tf_op jit(solution)/shard_map/while/body/eval_jaxpr/reduce_scatter | solution.py:258
  791.0 174.7 %reduce-scatter.3.cloned.1.call-done = f32[48,3072]{1,0:T(8,128)} async-done(((f32[768,3072]{1,0:T(8,128)}), f32[48,3072]{1,0:T(8,128)}) %reduce-scatter.3.cloned.1.call-update) | async-done | bytes 589840 | tf_op jit(solution)/shard_map/while/body/eval_jaxpr/reduce_scatter | solution.py:256
  975.2 75.5 %all-gather.3.cloned.1.call-done = bf16[1,768,3072]{2,1,0:T(8,128)(2,1)} async-done(((bf16[1,48,3072]{2,1,0:T(8,128)(2,1)}), bf16[1,768,3072]{2,1,0:T(8,128)(2,1)}) %all-gather.3.cloned.1.call-update) | async-done | bytes 4718608 | tf_op jit(solution)/shard_map/while/body/eval_jaxpr/all_gather | solution.py:251
  1050.8 78.0 %conditional.9 = (bf16[1024,768]{1,0:T(8,128)(2,1)}, bf16[1024,2304]{1,0:T(8,128)(2,1)}, f32[3,4,1024]{2,1,0:T(4,128)}, f32[1024,768]{0,1:T(8,128)}) conditional(s32[]{:T(128)} %convert_element_type.274, () %tuple.157, (bf16[1024,768]{1,0:T(8,128)(2,1)S(1)}, f32[1024]{0:T(1024)}, f32[768]{0:T(1024)S(1)}, f32[768]{0:T(1024)S(1)}, ...), branch_computations={%region_3.3_spmd, %region_4.12_spmd} | conditional | flops 5981080064 | bytes 124040616 | solution.py:308
  1071.5 47.5 %while.67 = (s32[]{:T(128)}, f32[3,1024,256]{1,2,0:T(8,128)}, f32[3,4,1024]{2,1,0:T(4,128)}, bf16[3,1024,256]{1,2,0:T(8,128)(2,1)}, pred[1024,1024]{0,1:T(8,128)...) while((s32[]{:T(128)}, f32[3,1024,256]{1,2,0:T(8,128)}, ...), condition=%wide.region_10.9_spmd, body=%wide.region_7.8_spmd.sunk | while | flops 1124069376 | bytes 61472876 | solution.py:97
  1143.5 124.7 %collective-permute-done.1 = bf16[2,1024,768]{2,1,0:T(8,128)(2,1)} collective-permute-done((bf16[2,1024,768]{2,1,0:T(8,128)(2,1)S(1)}, bf16[2,1024,768]{2,1,0:T(8,128)(2,1)}, u32[]{:S(2)}, u32[]{:S(2)}) %collective-permute-start.1) | collective-permute-done | bytes 3145760 | tf_op jit(solution)/shard_map/while/body/eval_jaxpr/ppermute | solution.py:15
  1268.3 202.0 %conditional.11 = (f32[768,3072]{1,0:T(8,128)}, f32[768]{0:T(1024)}, f32[768]{0:T(1024)}, f32[768]{0:T(1024)}, f32[768]{0:T(1024)}, /*index=5*/f32[768]{0:T(1024...) conditional(s32[]{:T(128)} %convert_element_type.274, () %tuple.156, (bf16[1024,768]{1,0:T(8,128)(2,1)S(1)}, ...), branch_computations={%region_29.29_spmd, %region_30.47_spmd} | conditional | flops 12495356928 | bytes 345922368 | solution.py:323
  1300.7 136.8 %while.68 = (s32[]{:T(128)}, bf16[3,1024,256]{1,2,0:T(8,128)(2,1)}, bf16[3,1024,256]{1,2,0:T(8,128)(2,1)}, bf16[3,1024,256]{1,2,0:T(8,128)(2,1)}, bf16[3,1024,25...) while((s32[]{:T(128)}, bf16[3,1024,256]{1,2,0:T(8,128)(2,1)}, ...), condition=%wide.region_39.38_spmd, body=%wide.region_37.37_spmd.sunk | while | flops 2723147776 | bytes 191971664 | solution.py:160
  1309.5 11.3 multiply_reduce_fusion.8
  1400.7 11.3 multiply_reduce_fusion.8
  1489.4 109.6 %all-reduce.18.cloned.1.call-done = (f32[768]{0:T(1024)}, f32[768]{0:T(1024)}, f32[768]{0:T(1024)}, f32[768]{0:T(1024)}, f32[768]{0:T(1024)}, /*index=5*/f32[768...) async-done(((f32[768]{0:T(1024)}, f32[768]{0:T(1024)}, f32[768]{0:T(1024)}, ...) | async-done | bytes 67600 | tf_op jit(solution)/shard_map/while
  1604.6 141.1 %reduce-scatter.5.cloned.1.call-done = f32[96,768]{1,0:T(8,128)} async-done(((f32[3072,768]{1,0:T(8,128)}), f32[96,768]{1,0:T(8,128)}) %reduce-scatter.5.cloned.1.call-update) | async-done | bytes 294928 | tf_op jit(solution)/shard_map/while/body/eval_jaxpr/reduce_scatter | solution.py:258
  1746.7 174.7 %reduce-scatter.3.cloned.1.call-done = f32[48,3072]{1,0:T(8,128)} async-done(((f32[768,3072]{1,0:T(8,128)}), f32[48,3072]{1,0:T(8,128)}) %reduce-scatter.3.cloned.1.call-update) | async-done | bytes 589840 | tf_op jit(solution)/shard_map/while/body/eval_jaxpr/reduce_scatter | solution.py:256
  (668 shorter events, 614.3 us)
Async XLA Ops:
  7.6 86.8 %all-gather.3.cloned.1.call-start = ((), (), s32[]{:S(2)}) async-start(), calls=%async_computation.2 | async-start | bytes 5013504 | tf_op jit(solution)/shard_map/while/body/eval_jaxpr/all_gather | solution.py:251
  8.4 166.6 %all-gather.5.cloned.1.call-start = ((), (), s32[]{:S(2)}) async-start(), calls=%async_computation.3 | async-start | bytes 4866048 | tf_op jit(solution)/shard_map/while/body/eval_jaxpr/all_gather | solution.py:252
  9.1 634.2 %all-reduce.18.cloned.1.call-start = ((), (), s32[]{:S(2)}) async-start(), calls=%async_computation.6 | async-start | bytes 155648 | tf_op jit(solution)/shard_map/while
  172.6 4.6 collective-permute-start
  186.1 126.4 %collective-permute-start.1 = (bf16[2,1024,768]{2,1,0:T(8,128)(2,1)S(1)}, bf16[2,1024,768]{2,1,0:T(8,128)(2,1)}, u32[]{:S(2)}, u32[]{:S(2)}) collective-permute-start(bf16[2,1024,768]{2,1,0:T(8,128)(2,1)S(1)} %get-tuple-element.1238), channel_id=1, source_target_pairs={{16,0},{17,1},{18,2},{19,3},{20,4},{21,5},{22,6},{23,7},{24,8},{25... | collective-permute-start | bytes 9437192 | tf_op jit(solution)/shard_map/while/body/eval_jaxpr/ppermute | solution.py:15
  514.7 275.3 %reduce-scatter.5.cloned.1.call-start = ((), (), s32[]{:S(2)}) async-start(), calls=%async_computation.5 | async-start | bytes 9732096 | tf_op jit(solution)/shard_map/while/body/eval_jaxpr/reduce_scatter | solution.py:258
  515.3 450.4 %reduce-scatter.3.cloned.1.call-start = ((), (), s32[]{:S(2)}) async-start(), calls=%async_computation.4 | async-start | bytes 10027008 | tf_op jit(solution)/shard_map/while/body/eval_jaxpr/reduce_scatter | solution.py:256
  527.1 438.7 %copy-start.24 = (f32[48,3072]{1,0:T(8,128)S(1)}, f32[48,3072]{1,0:T(8,128)}, u32[]{:S(2)}) copy-start(f32[48,3072]{1,0:T(8,128)} %get-tuple-element.1457) | copy-start | bytes 1769476 | tf_op jit(solution)/shard_map/while
  644.1 322.9 %copy-start.51 = (f32[96]{0:T(128)}, f32[96]{0:T(128)S(1)}, u32[]{:S(2)}) copy-start(f32[96]{0:T(128)S(1)} %fusion.176) | copy-start | bytes 1156 | tf_op jit(solution)/shard_map/while
  644.9 322.1 %copy-start.55 = (f32[96]{0:T(128)}, f32[96]{0:T(128)S(1)}, u32[]{:S(2)}) copy-start(f32[96]{0:T(128)S(1)} %get-tuple-element.1511) | copy-start | bytes 1156 | tf_op jit(solution)/shard_map/while
  644.9 322.1 %copy-start.57 = (f32[96]{0:T(128)}, f32[96]{0:T(128)S(1)}, u32[]{:S(2)}) copy-start(f32[96]{0:T(128)S(1)} %get-tuple-element.1510) | copy-start | bytes 1156 | tf_op jit(solution)/shard_map/while
  645.7 321.3 %copy-start.75 = (f32[24]{0:T(128)}, f32[24]{0:T(128)S(1)}, u32[]{:S(2)}) copy-start(f32[24]{0:T(128)S(1)} %get-tuple-element.1501) | copy-start | bytes 292 | tf_op jit(solution)/shard_map/while
  968.0 82.7 %all-gather.3.cloned.1.call-start = ((), (), s32[]{:S(2)}) async-start(), calls=%async_computation.2 | async-start | bytes 5013504 | tf_op jit(solution)/shard_map/while/body/eval_jaxpr/all_gather | solution.py:251
  968.6 162.6 %all-gather.5.cloned.1.call-start = ((), (), s32[]{:S(2)}) async-start(), calls=%async_computation.3 | async-start | bytes 4866048 | tf_op jit(solution)/shard_map/while/body/eval_jaxpr/all_gather | solution.py:252
  969.3 629.7 %all-reduce.18.cloned.1.call-start = ((), (), s32[]{:S(2)}) async-start(), calls=%async_computation.6 | async-start | bytes 155648 | tf_op jit(solution)/shard_map/while
  1128.8 4.6 collective-permute-start
  1142.2 126.0 %collective-permute-start.1 = (bf16[2,1024,768]{2,1,0:T(8,128)(2,1)S(1)}, bf16[2,1024,768]{2,1,0:T(8,128)(2,1)}, u32[]{:S(2)}, u32[]{:S(2)}) collective-permute-start(bf16[2,1024,768]{2,1,0:T(8,128)(2,1)S(1)} %get-tuple-element.1238), channel_id=1, source_target_pairs={{16,0},{17,1},{18,2},{19,3},{20,4},{21,5},{22,6},{23,7},{24,8},{25... | collective-permute-start | bytes 9437192 | tf_op jit(solution)/shard_map/while/body/eval_jaxpr/ppermute | solution.py:15
  1470.4 275.3 %reduce-scatter.5.cloned.1.call-start = ((), (), s32[]{:S(2)}) async-start(), calls=%async_computation.5 | async-start | bytes 9732096 | tf_op jit(solution)/shard_map/while/body/eval_jaxpr/reduce_scatter | solution.py:258
  1471.1 450.4 %reduce-scatter.3.cloned.1.call-start = ((), (), s32[]{:S(2)}) async-start(), calls=%async_computation.4 | async-start | bytes 10027008 | tf_op jit(solution)/shard_map/while/body/eval_jaxpr/reduce_scatter | solution.py:256
  1482.9 438.6 %copy-start.24 = (f32[48,3072]{1,0:T(8,128)S(1)}, f32[48,3072]{1,0:T(8,128)}, u32[]{:S(2)}) copy-start(f32[48,3072]{1,0:T(8,128)} %get-tuple-element.1457) | copy-start | bytes 1769476 | tf_op jit(solution)/shard_map/while
  1599.8 322.9 %copy-start.51 = (f32[96]{0:T(128)}, f32[96]{0:T(128)S(1)}, u32[]{:S(2)}) copy-start(f32[96]{0:T(128)S(1)} %fusion.176) | copy-start | bytes 1156 | tf_op jit(solution)/shard_map/while
  1600.6 322.1 %copy-start.55 = (f32[96]{0:T(128)}, f32[96]{0:T(128)S(1)}, u32[]{:S(2)}) copy-start(f32[96]{0:T(128)S(1)} %get-tuple-element.1511) | copy-start | bytes 1156 | tf_op jit(solution)/shard_map/while
  1600.6 322.1 %copy-start.57 = (f32[96]{0:T(128)}, f32[96]{0:T(128)S(1)}, u32[]{:S(2)}) copy-start(f32[96]{0:T(128)S(1)} %get-tuple-element.1510) | copy-start | bytes 1156 | tf_op jit(solution)/shard_map/while
  1927.1 4.3 collective-permute-start.2
  (173 other events, 15883.6 us)
Sparse Core Ops, SparseCore 0:
  11.3 83.1 all-gather.2
  97.4 62.1 all-gather.4
  514.8 128.4 all-reduce.17
  651.6 138.3 reduce-scatter.4
  795.5 170.1 reduce-scatter.2
  971.3 79.3 all-gather.2
  1053.6 62.1 all-gather.4
  1470.5 128.4 all-reduce.17
  1607.3 138.3 reduce-scatter.4
  1751.2 170.1 reduce-scatter.2
where the time goes:
time: 1950 us; the launch traced here: 1940 us
  waiting for transfers between devices  1270 us (65%)
  matrix products  288 us (15%)
  other arithmetic  212 us (11%)
  local copies, waits for them, and re-layouts  133 us (7%)
    reduce_scatter x2, waiting for transfers between devices, spread(): lax.psum_scatter(grad_block, 'dp', scatter_dimension=0, tiled=True)  349 us
    reduce_scatter x2, waiting for transfers between devices, spread(): lax.psum_scatter(grad_down, ('section', 'dp'), scatter_dimension=0, tiled...  282 us
    ppermute x5, waiting for transfers between devices, passed_along(): lax.ppermute(value, axis, [(source, source + steps) for source in range(f...  257 us
    while x12, waiting for transfers between devices  223 us
    all_gather x2, waiting for transfers between devices, fetch(): block = lax.all_gather(half_weights, 'dp', axis=1, tiled=True)[0]  155 us
    dot_general x12, matrix products, masked_scores(): jnp.einsum('qhd,khd->hqk', per_head(query), per_head(key), preferred_elem...  87.8 us
    convert_element_type x6, other arithmetic, one_group(): grad_scores = (soft * (grad_soft - inner)).astype(jnp.bfloat16)  62.5 us
    dot_general x6, matrix products, one_group(): jnp.einsum('hqk,qhd->khd', soft.astype(jnp.bfloat16), grad_heads, preferr...  52.4 us
  transfers between devices with their start and end apart: 15, of which 13 were waited for; matrix products, arithmetic and copies ran while one was open for 11% of the time, Pallas kernels for 0%

commit v1 on v0

--- a/solution.py
+++ b/solution.py
@@ -7,12 +7,6 @@
 
 
 EPS = 1e-05
-
-
-def passed_along(value, axis, steps):
-    count = lax.axis_size(axis)
-    first, last = (max(0, -steps), min(count, count - steps))
-    return lax.ppermute(value, axis, [(source, source + steps) for source in range(first, last)])
 
 
 def layer_norm(value, gain, shift):
@@ -27,7 +21,8 @@
 
 
 def row_masks(lengths_row, count):
-    ends = jnp.cumsum(lengths_row)
+    slots = jnp.arange(lengths_row.shape[0], dtype=jnp.int32)
+    ends = jnp.sum(jnp.where(slots[:, None] <= slots[None, :], lengths_row[:, None], 0), axis=0)
     index = jnp.arange(count, dtype=jnp.int32)
     segment = jnp.sum((index[:, None] >= ends[None, :]).astype(jnp.int32), axis=1)
     alive = segment < lengths_row.shape[0]
@@ -222,159 +217,83 @@
     seq_lengths,
     half_weights,
     down_weight,
-    pre_gain,
-    pre_shift,
-    query_bias,
-    value_bias,
-    sub_gain,
-    sub_shift,
-    out_bias,
-    ffn_gain,
-    ffn_shift,
-    up_bias,
-    mid_gain,
-    mid_shift,
-    down_bias,
+    *all_vectors,
 ):
-    first = lax.axis_index("section") == 0
+    section = lax.axis_index("section")
+    sections = lax.axis_size("section")
+    both = ("section", "dp")
     width = tokens.shape[1]
     batches = seq_lengths.shape[0]
     count = tokens.shape[0] // batches
+    own_batches = batches // sections
+    own_rows = own_batches * count
     hidden_units = half_weights.shape[2]
-    groups = width // (4 * HEAD_DIM)
-    shares = lax.axis_size("section") * lax.axis_size("dp")
-    attention_vectors = (pre_gain, pre_shift, query_bias, value_bias, sub_gain, sub_shift, out_bias)
-    ffn_vectors = (ffn_gain, ffn_shift, up_bias, mid_gain, mid_shift, down_bias)
-    all_vectors = attention_vectors + ffn_vectors
-
-    def fetch():
-        block = lax.all_gather(half_weights, "dp", axis=1, tiled=True)[0]
-        down_full = lax.all_gather(down_weight, ("section", "dp"), axis=0, tiled=True)
-        return (block, down_full)
-
-    def spread(grad_block, grad_down, vectors):
-        block_part = lax.psum_scatter(grad_block, "dp", scatter_dimension=0, tiled=True)
-        parts = (
-            lax.psum_scatter(grad_down, ("section", "dp"), scatter_dimension=0, tiled=True),
-            lax.psum_scatter(vectors[0], ("section", "dp"), scatter_dimension=0, tiled=True),
-            lax.psum_scatter(vectors[1], ("section", "dp"), scatter_dimension=0, tiled=True),
-            lax.psum_scatter(vectors[2], ("section", "dp"), scatter_dimension=0, tiled=True),
-            lax.psum_scatter(vectors[3], ("section", "dp"), scatter_dimension=0, tiled=True),
-            lax.psum_scatter(vectors[4], ("section", "dp"), scatter_dimension=0, tiled=True),
-            lax.psum_scatter(vectors[5], ("section", "dp"), scatter_dimension=0, tiled=True),
-            lax.psum_scatter(vectors[6], ("section", "dp"), scatter_dimension=0, tiled=True),
-            lax.psum_scatter(vectors[7], ("section", "dp"), scatter_dimension=0, tiled=True),
-            lax.psum_scatter(vectors[8], ("section", "dp"), scatter_dimension=0, tiled=True),
-            lax.psum_scatter(vectors[9], ("section", "dp"), scatter_dimension=0, tiled=True),
-            lax.psum_scatter(vectors[10], ("section", "dp"), scatter_dimension=0, tiled=True),
-            lax.psum_scatter(vectors[11], ("section", "dp"), scatter_dimension=0, tiled=True),
-            lax.psum_scatter(vectors[12], ("section", "dp"), scatter_dimension=0, tiled=True),
-        )
-        return (block_part, parts[0], tuple(parts[1:]))
-
-    initial = (
-        jnp.zeros((half_weights.shape[1], hidden_units), jnp.float32),
-        jnp.zeros(down_weight.shape, jnp.float32),
-        tuple((jnp.zeros((vector.shape[0] // shares,), jnp.float32) for vector in all_vectors)),
-    )
-
-    def spare_forward():
-        return (
-            jnp.zeros((count, width), jnp.bfloat16),
-            jnp.zeros((count, 3 * width), jnp.bfloat16),
-            jnp.zeros((groups, 4, count), jnp.float32),
-            jnp.zeros((count, width), jnp.float32),
-        )
-
-    def spare_ffn():
-        return (
-            jnp.zeros((2, count, width), jnp.bfloat16),
-            jnp.zeros((width, hidden_units), jnp.float32),
-            jnp.zeros((hidden_units, width), jnp.float32),
-            tuple((jnp.zeros(vector.shape, jnp.float32) for vector in ffn_vectors)),
-        )
-
-    def spare_backward():
-        return (
-            jnp.zeros((count, width), jnp.float32),
-            jnp.zeros((width, hidden_units), jnp.float32),
-            tuple((jnp.zeros(vector.shape, jnp.float32) for vector in attention_vectors)),
-        )
-
-    def step(carry, inputs):
-        x_block, dy_block, lengths_row = inputs
-        block, down_full = fetch()
-        alive, allowed = row_masks(lengths_row, count)
-        hidden, projected, logsum, context = lax.cond(
-            first,
-            lambda: attention_forward(x_block, alive, allowed, block, attention_vectors),
-            spare_forward,
-        )
-        arrived = passed_along(hidden, "section", 1)
-        stacked, grad_up, grad_down, ffn_small = lax.cond(
-            first,
-            spare_ffn,
-            lambda: feed_forward(arrived, dy_block, alive, block, down_full, ffn_vectors),
-        )
-        returned = passed_along(stacked, "section", -1)
-        residual = jnp.where(first, hidden, arrived).astype(jnp.float32)
-        branch = jnp.where(first, returned[0], stacked[0]).astype(jnp.float32)
-        out_block = residual + alive[:, None] * branch
-        grad_x, grad_attention, attention_small = lax.cond(
-            first,
-            lambda: attention_backward(
-                x_block,
-                alive,
-                allowed,
-                block,
-                attention_vectors,
-                projected,
-                logsum,
-                context,
-                returned[1],
-            ),
-            spare_backward,
-        )
-        grad_block = jnp.where(first, grad_attention, grad_up)
-        vectors = attention_small + ffn_small
-        block_part, down_part, vector_parts = spread(grad_block, grad_down, vectors)
-        carry = jax.tree.map(
-            lambda total, extra: total + extra, carry, (block_part, down_part, vector_parts)
-        )
-        return (carry, (out_block, grad_x))
-
-    shaped = (
-        tokens.reshape(batches, count, width),
-        out_grad.reshape(batches, count, width),
-        seq_lengths,
-    )
-    carry, (outputs, grads) = lax.scan(step, initial, shaped)
-    block_part, down_part, vector_parts = carry
-    grad_rows = grads.reshape(-1, width)
-    half_width = width // 2
-    partner_rows = passed_along(
-        grad_rows[:, half_width:].astype(jnp.bfloat16), "section", 1
-    ).astype(jnp.float32)
-    tokens_grad = jnp.where(first, grad_rows[:, :half_width], partner_rows)
-    return (
-        outputs.reshape(-1, width),
-        tokens_grad,
-        block_part[None],
-        down_part,
-        vector_parts[0],
-        vector_parts[1],
-        vector_parts[2],
-        vector_parts[3],
-        vector_parts[4],
-        vector_parts[5],
-        vector_parts[6],
-        vector_parts[7],
-        vector_parts[8],
-        vector_parts[9],
-        vector_parts[10],
-        vector_parts[11],
-        vector_parts[12],
-    )
+    shares = sections * lax.axis_size("dp")
+    attention_vectors = all_vectors[:7]
+    ffn_vectors = all_vectors[7:]
+
+    blocks = lax.all_gather(half_weights[0], both, axis=0, tiled=True)
+    blocks = blocks.reshape(sections, width, hidden_units)
+    down_full = lax.all_gather(down_weight, both, axis=0, tiled=True)
+    attention_block, up_block = blocks[0], blocks[1]
+
+    def own(array, rows):
+        return lax.dynamic_slice_in_dim(array, section * rows, rows, axis=0)
+
+    x_rows = own(tokens, own_rows)
+    dy_rows = own(out_grad, own_rows)
+    lengths = own(seq_lengths, own_batches)
+
+    def step(index):
+        x_block = x_rows[index * count : (index + 1) * count]
+        dy_block = dy_rows[index * count : (index + 1) * count]
+        alive, allowed = row_masks(lengths[index], count)
+        hidden, projected, logsum, context = attention_forward(
+            x_block, alive, allowed, attention_block, attention_vectors
+        )
+        stacked, grad_up, grad_down, ffn_small = feed_forward(
+            hidden, dy_block, alive, up_block, down_full, ffn_vectors
+        )
+        out_block = hidden.astype(jnp.float32) + alive[:, None] * stacked[0].astype(jnp.float32)
+        grad_x, grad_attention, attention_small = attention_backward(
+            x_block,
+            alive,
+            allowed,
+            attention_block,
+            attention_vectors,
+            projected,
+            logsum,
+            context,
+            stacked[1],
+        )
+        return (out_block, grad_x), (grad_attention, grad_up, grad_down, attention_small + ffn_small)
+
+    rows, sums = step(0)
+    outputs, grads = [rows[0]], [rows[1]]
+    for index in range(1, own_batches):
+        rows, more = step(index)
+        outputs.append(rows[0])
+        grads.append(rows[1])
+        sums = jax.tree.map(lambda total, extra: total + extra, sums, more)
+    out_block = jnp.concatenate(outputs, axis=0)
+    grad_rows = jnp.concatenate(grads, axis=0)
+    grad_attention, grad_up, grad_down, vectors = sums
+
+    block_part = lax.psum_scatter(
+        jnp.concatenate([grad_attention, grad_up], axis=0), both, scatter_dimension=0, tiled=True
+    )
+    down_part = lax.psum_scatter(grad_down, both, scatter_dimension=0, tiled=True)
+    packed = jnp.concatenate([vector.reshape(shares, -1) for vector in vectors], axis=1)
+    packed = lax.psum_scatter(packed, both, scatter_dimension=0, tiled=True).reshape(-1)
+    parts, start = [], 0
+    for vector in vectors:
+        size = vector.shape[0] // shares
+        parts.append(packed[start : start + size])
+        start += size
+
+    layer_out = lax.all_gather(out_block, "section", axis=0, tiled=True)
+    tokens_grad = lax.all_to_all(grad_rows, "section", split_axis=1, concat_axis=0, tiled=True)
+    return (layer_out, tokens_grad, block_part[None], down_part, *parts)
 
 
 def solution(mesh):

time: 1950 us -> 940 us (0.48)
  waiting for transfers between devices: 1270 us -> 504 us
  other arithmetic: 212 us -> 106 us
  local copies, waits for them, and re-layouts: 133 us -> 68.8 us
  matrix products: 288 us -> 233 us
    reduce_scatter x4 -> x2, waiting for transfers between devices: 632 us -> 349 us  [the longest x1 212 us: shards(): lax.psum_scatter(jnp.concatenate([grad_attention, grad_up], axis=0), both...]
    ppermute x5 -> x0, waiting for transfers between devices: 257 us -> none  [passed_along(): lax.ppermute(value, axis, [(source, source + steps) for source in range(f...]
    while x12 -> x0, waiting for transfers between devices: 223 us -> none
    unnamed x0 -> x7, waiting for transfers between devices: none -> 62.4 us
    all_gather x4 -> x3, waiting for transfers between devices: 155 us -> 92.8 us  [the longest x1 75.7 us: shards(): blocks = lax.all_gather(half_weights[0], both, axis=0, tiled=True)]
    dot_general x0 -> x2, matrix products: none -> 47.7 us  [the longest x1 37.6 us: feed_forward(): jnp.dot(normed, up_weight, preferred_element_type=jnp.float32) + up_bias]
    dot_general x12 -> x6, matrix products: 87.8 us -> 43.1 us  [masked_scores(): jnp.einsum('qhd,khd->hqk', per_head(query), per_head(key), preferred_elem...]
    convert_element_type x6 -> x3, other arithmetic: 62.5 us -> 23.6 us  [one_group(): grad_scores = (soft * (grad_soft - inner)).astype(jnp.bfloat16)]
  transfers between devices with their start and end apart: 15 -> 6, of which waited for: 13 -> 5; matrix products, arithmetic and copies ran while one was open for 11% -> 19% of each run, Pallas kernels for 0% -> 0%
where the time goes in v1:
time: 940 us; the launch traced here: 935 us
  waiting for transfers between devices  504 us (54%)
  matrix products  233 us (25%)
  other arithmetic  106 us (11%)
  local copies, waits for them, and re-layouts  68.8 us (7%)
  between operations  15.4 us (2%)
    reduce_scatter x1, waiting for transfers between devices, shards(): lax.psum_scatter(jnp.concatenate([grad_attention, grad_up], axis=0), both...  212 us
    reduce_scatter x1, waiting for transfers between devices, shards(): lax.psum_scatter(grad_down, both, scatter_dimension=0, tiled=True)  136 us
    all_gather x1, waiting for transfers between devices, shards(): blocks = lax.all_gather(half_weights[0], both, axis=0, tiled=True)  75.7 us
    unnamed x7, waiting for transfers between devices  62.4 us
    dot_general x4, matrix products, contract_cols(): lax.dot_general(left, right, (((1,), (1,)), ((), ())), preferred_element_...  46.4 us
    dot_general x6, matrix products, masked_scores(): jnp.einsum('qhd,khd->hqk', per_head(query), per_head(key), preferred_elem...  43.1 us
    dot_general x1, matrix products, feed_forward(): jnp.dot(normed, up_weight, preferred_element_type=jnp.float32) + up_bias  37.6 us
    dot_general x3, matrix products, one_group(): jnp.einsum('hqk,qhd->khd', soft.astype(jnp.bfloat16), grad_heads, preferr...  25.8 us
  transfers between devices with their start and end apart: 6, of which 5 were waited for; matrix products, arithmetic and copies ran while one was open for 19% of the time, Pallas kernels for 0%

profile of v1, /device:TPU:0, one launch (start us, length us, event | category | flops | bytes accessed | tf_op | source)
XLA Modules:
  0.0 934.9 jit_solution(17875908142567261711)
XLA Ops:
  20.0 75.7 %all-gather.9.cloned.1.call-done = bf16[1,1536,3072]{2,1,0:T(8,128)(2,1)} async-done(((bf16[1,48,3072]{2,1,0:T(8,128)(2,1)}), bf16[1,1536,3072]{2,1,0:T(8,128)(2,1)}) %all-gather.9.cloned.1.call-update) | async-done | bytes 9437200 | tf_op jit(solution)/shard_map/all_gather | solution.py:235
  111.2 51.2 %while.30 = (s32[]{:T(128)}, f32[3,1024,256]{1,2,0:T(8,128)S(1)}, f32[3,4,1024]{2,1,0:T(4,128)}, bf16[3,1024,256]{1,2,0:T(8,128)(2,1)}, bf16[3,1024,256]{1,2,0:T...) while((s32[]{:T(128)}, f32[3,1024,256]{1,2,0:T(8,128)S(1)}, ...), condition=%wide.region_7.8_spmd.clone.clone, body=%wide.region_4.7_spmd.clone.sunk.clone | while | flops 1130360832 | bytes 62527072 | solution.py:92
  170.0 37.6 %fusion.85 = (f32[1024]{0:T(1024)S(1)}, f32[1024,3072]{1,0:T(8,128)}, f32[1024,3072]{1,0:T(8,128)}, f32[1024,3072]{1,0:T(8,128)}) fusion(f32[3072]{0:T(1024)S(1)} %copy-done.60, bf16[1,1536,3072]{2,1,0:T(8,128)(2,1)S(1)} %bitcast.238, bf16[1024,768]{0,1:T(8,128)(2,1)S(1)} %get-tuple-element.326, f32[768]{0:T(1024)S(1)} %copy-done.72, ...), kind=kOutput, calls=%fused_computation.181 | convolution fusion | flops 5044173824 | bytes 44072960 | tf_op jit(solution)/shard_map/dot_general | solution.py:184
  207.6 24.2 %multiply_reduce_fusion.2 = (f32[1024]{0:T(1024)S(1)}, f32[1024]{0:T(1024)S(1)}, f32[3072]{0:T(1024)}, f32[1024,3072]{1,0:T(8,128)}) fusion(f32[1024,3072]{1,0:T(8,128)} %get-tuple-element.289, f32[3072]{0:T(1024)S(1)} %copy-done.37, f32[1024]{0:T(1024)S(1)} %broadcast_multiply_fusion, bf16[3072,768]{1,0:T(8,128)(2,1)} %all-gather.5.cloned.1.call-done, ...), kind=kOutput, calls=%fused_computation.47 | convolution fusion | flops 4856212480 | bytes 31498240 | tf_op jit(solution)/shard_map/dot_general | solution.py:61
  231.9 8.4 multiply_reduce_fusion.1
  240.3 19.4 %convert_reduce_fusion = (f32[3072]{0:T(1024)}, bf16[1024,3072]{1,0:T(8,128)(2,1)S(1)}, bf16[1024,3072]{1,0:T(8,128)(2,1)}) fusion(f32[1024,3072]{1,0:T(8,128)} %get-tuple-element.290, f32[1024]{0:T(1024)S(1)} %negate_multiply_fusion.4, f32[1024]{0:T(1024)S(1)} %get-tuple-element.323, f32[1024,3072]{1,0:T(8,128)S(1)} %bitcast.214, ...), kind=kLoop, calls=%fused_computation.45 | loop fusion | flops 88077312 | bytes 62980096 | tf_op jit(solution)/shard_map/reduce_sum | solution.py:199
  259.8 9.9 %fusion.81 = (f32[768]{0:T(1024)}, f32[1024]{0:T(1024)S(1)}, f32[1024,768]{0,1:T(8,128)S(1)}) fusion(f32[768]{0:T(1024)S(1)} %copy-done.50, f32[1024]{0:T(1024)S(1)} %broadcast_multiply_fusion.1, bf16[1024,768]{0,1:T(8,128)(2,1)S(1)} %get-tuple-element.326, bf16[1024,3072]{1,0:T(8,128)(2,1)S(1)} %get-tuple-element.286, ...), kind=kOutput, calls=%fused_computation.178 | convolution fusion | flops 4836554752 | bytes 15742976 | tf_op jit(solution)/shard_map/dot_general | solution.py:61
  281.0 136.1 %while.31 = (s32[]{:T(128)}, bf16[3,1024,256]{1,2,0:T(8,128)(2,1)}, bf16[3,1024,256]{1,2,0:T(8,128)(2,1)}, bf16[3,1024,256]{1,2,0:T(8,128)(2,1)}, bf16[3,1024,25...) while((s32[]{:T(128)}, bf16[3,1024,256]{1,2,0:T(8,128)(2,1)}, ...), condition=%wide.region_22.23_spmd.clone.clone, body=%wide.region_20.22_spmd.clone.sunk.clone | while | flops 2729439232 | bytes 222386480 | solution.py:155
  292.3 11.1 %multiply_reduce_fusion.8 = (f32[4,1024]{1,0:T(4,128)}, f32[4,1024,1024]{1,2,0:T(8,128)}) fusion(f32[4,1024,1024]{1,2,0:T(8,128)S(1)} %fusion.169, f32[4,1024]{1,0:T(4,128)} %dynamic-slice_bitcast_fusion.16, bf16[1024,4,64]{0,2,1:T(8,128)(2,1)} %bitcast.205, bf16[1024,4,64]{0,2,1:T(8,128)(2,1)S(1)} %bitcast.203, pred[1024,1024]{0,1:T(8,128)(4,1)} %fusion.170), kind=kOutput, calls=%fused_computation.21.clone.1.clone | convolution fusion | flops 557838336 | bytes 35684352 | tf_op jit(solution)/shard_map/while/body/eval_jaxpr/qhd,khd->hqk/dot_general | solution.py:48
  303.4 7.9 multiply_convert_fusion.3
  314.5 8.6 fusion.171
  337.5 11.1 %multiply_reduce_fusion.8 = (f32[4,1024]{1,0:T(4,128)}, f32[4,1024,1024]{1,2,0:T(8,128)}) fusion(f32[4,1024,1024]{1,2,0:T(8,128)S(1)} %fusion.169, f32[4,1024]{1,0:T(4,128)} %dynamic-slice_bitcast_fusion.16, bf16[1024,4,64]{0,2,1:T(8,128)(2,1)} %bitcast.205, bf16[1024,4,64]{0,2,1:T(8,128)(2,1)S(1)} %bitcast.203, pred[1024,1024]{0,1:T(8,128)(4,1)} %fusion.170), kind=kOutput, calls=%fused_computation.21.clone.1.clone | convolution fusion | flops 557838336 | bytes 35684352 | tf_op jit(solution)/shard_map/while/body/eval_jaxpr/qhd,khd->hqk/dot_general | solution.py:48
  348.6 7.9 multiply_convert_fusion.3
  359.7 8.6 fusion.171
  382.7 11.1 %multiply_reduce_fusion.8 = (f32[4,1024]{1,0:T(4,128)}, f32[4,1024,1024]{1,2,0:T(8,128)}) fusion(f32[4,1024,1024]{1,2,0:T(8,128)S(1)} %fusion.169, f32[4,1024]{1,0:T(4,128)} %dynamic-slice_bitcast_fusion.16, bf16[1024,4,64]{0,2,1:T(8,128)(2,1)} %bitcast.205, bf16[1024,4,64]{0,2,1:T(8,128)(2,1)S(1)} %bitcast.203, pred[1024,1024]{0,1:T(8,128)(4,1)} %fusion.170), kind=kOutput, calls=%fused_computation.21.clone.1.clone | convolution fusion | flops 557838336 | bytes 35684352 | tf_op jit(solution)/shard_map/while/body/eval_jaxpr/qhd,khd->hqk/dot_general | solution.py:48
  404.9 8.6 fusion.171
  420.9 8.3 fusion.83
  434.4 10.2 %convert_add_fusion = f32[1024,768]{0,1:T(8,128)} fusion(bf16[1024,768]{0,1:T(8,128)(2,1)} %copy-done.13, f32[1024]{0:T(1024)S(1)} %copy-done.59, f32[768]{0:T(1024)S(1)} %copy-done.69, bf16[1024,3072]{1,0:T(8,128)(2,1)} %get-tuple-element.301, bf16[3072,768]{1,0:T(8,128)(2,1)} %all-gather.5.cloned.1.call-done), kind=kOutput, calls=%fused_computation.70 | convolution fusion | flops 4836556800 | bytes 15735808 | tf_op jit(solution)/shard_map/dot_general | solution.py:188
  444.6 9.9 %fusion.61 = f32[3072,768]{1,0:T(8,128)} fusion(bf16[1024,3072]{1,0:T(8,128)(2,1)} %get-tuple-element.301, bf16[1024,768]{0,1:T(8,128)(2,1)} %copy.94, f32[1024]{0:T(1024)S(1)} %copy-done.59), kind=kOutput, calls=%fused_computation.126 | convolution fusion | flops 4834197504 | bytes 17305600 | tf_op jit(solution)/shard_map/dot_general | solution.py:55
  469.9 8.6 pad_maximum_fusion
  491.5 60.9 %all-reduce.3.cloned.1.call-done = f32[32,528]{1,0:T(8,128)} async-done(((f32[32,528]{1,0:T(8,128)}), f32[32,528]{1,0:T(8,128)}) %all-reduce.3.cloned.1.call-update) | async-done | bytes 67600
  555.4 17.2 %all-gather.7.cloned.1.call-done = f32[2048,768]{0,1:T(8,128)} async-done(((f32[1024,768]{0,1:T(8,128)}), f32[2048,768]{0,1:T(8,128)}) %all-gather.7.cloned.1.call-update) | async-done | bytes 6291472 | tf_op jit(solution)/shard_map/all_gather | solution.py:294
  579.3 136.3 %reduce-scatter.5.cloned.1.call-done = f32[96,768]{1,0:T(8,128)} async-done(((f32[3072,768]{1,0:T(8,128)}), f32[96,768]{1,0:T(8,128)}) %reduce-scatter.5.cloned.1.call-update) | async-done | bytes 294928 | tf_op jit(solution)/shard_map/reduce_scatter | solution.py:285
  715.6 212.2 %reduce-scatter.3.cloned.1.call-done = f32[48,3072]{1,0:T(8,128)} async-done(((f32[1536,3072]{1,0:T(8,128)}), f32[48,3072]{1,0:T(8,128)}) %reduce-scatter.3.cloned.1.call-update) | async-done | bytes 589840 | tf_op jit(solution)/shard_map/reduce_scatter | solution.py:282
  (328 shorter events, 205.0 us)
Async XLA Ops:
  7.2 88.5 %all-gather.9.cloned.1.call-start = ((), (), s32[]{:S(2)}) async-start(), calls=%async_computation.7 | async-start | bytes 9732096 | tf_op jit(solution)/shard_map/all_gather | solution.py:235
  7.9 199.6 %all-gather.5.cloned.1.call-start = ((), (), s32[]{:S(2)}) async-start(), calls=%async_computation.3 | async-start | bytes 4866048 | tf_op jit(solution)/shard_map/all_gather | solution.py:237
  8.7 543.7 %all-reduce.3.cloned.1.call-start = ((), (), s32[]{:S(2)}) async-start(), calls=%async_computation.8 | async-start | bytes 163840
  14.9 80.8 %copy-start.8 = (bf16[1024,768]{0,1:T(8,128)(2,1)}, bf16[1024,768]{0,1:T(8,128)(2,1)S(1)}, u32[]{:S(2)}) copy-start(bf16[1024,768]{0,1:T(8,128)(2,1)S(1)} %copy.93) | copy-start | bytes 4718596
  15.2 80.6 %copy-start.33 = (f32[1024]{0:T(1024)}, f32[1024]{0:T(1024)S(1)}, u32[]{:S(2)}) copy-start(f32[1024]{0:T(1024)S(1)} %broadcast_multiply_fusion.3) | copy-start | bytes 12292
  15.6 80.1 %copy-start.42 = (f32[1024]{0:T(1024)}, f32[1024]{0:T(1024)S(1)}, u32[]{:S(2)}) copy-start(f32[1024]{0:T(1024)S(1)} %fusion.69) | copy-start | bytes 12292
  16.8 78.9 %copy-start.52 = (f32[768]{0:T(1024)S(1)}, f32[768]{0:T(1024)}, u32[]{:S(2)}) copy-start(f32[768]{0:T(1024)} %param.27) | copy-start | bytes 9220
  16.8 78.9 %copy-start.70 = (f32[768]{0:T(1024)S(1)}, f32[768]{0:T(1024)}, u32[]{:S(2)}) copy-start(f32[768]{0:T(1024)} %param.28) | copy-start | bytes 9220
  169.4 102.2 %copy-start.13 = (bf16[1024,768]{0,1:T(8,128)(2,1)}, bf16[1024,768]{0,1:T(8,128)(2,1)S(1)}, u32[]{:S(2)}) copy-start(bf16[1024,768]{0,1:T(8,128)(2,1)S(1)} %get-tuple-element.326) | copy-start | bytes 4718596
  169.4 102.2 %copy-start.35 = (f32[1024]{0:T(1024)}, f32[1024]{0:T(1024)S(1)}, u32[]{:S(2)}) copy-start(f32[1024]{0:T(1024)S(1)} %broadcast_multiply_fusion.1) | copy-start | bytes 12292
  170.0 101.6 %copy-start.44 = (f32[1024]{0:T(1024)}, f32[1024]{0:T(1024)S(1)}, u32[]{:S(2)}) copy-start(f32[1024]{0:T(1024)S(1)} %fusion.71) | copy-start | bytes 12292
  170.0 37.6 %copy-start.37 = (f32[3072]{0:T(1024)S(1)}, f32[3072]{0:T(1024)}, u32[]{:S(2)}) copy-start(f32[3072]{0:T(1024)} %param.37) | copy-start | bytes 36868
  207.5 24.3 %slice-start = ((s8[12582912]{0:T(1024)(128)(4,1)}), s8[4194304]{0:T(1024)(128)(4,1)S(1)}, s32[]{:S(2)}) async-start(s8[12582912]{0:T(1024)(128)(4,1)} %bitcast.213), calls=%async_computation.9 | async-start | bytes 8388608
  207.6 24.3 %slice-start.1 = ((s8[12582912]{0:T(1024)(128)(4,1)}), s8[4194304]{0:T(1024)(128)(4,1)S(1)}, s32[]{:S(2)}) async-start(s8[12582912]{0:T(1024)(128)(4,1)} %bitcast.213), calls=%async_computation.10 | async-start | bytes 8388608
  207.6 24.3 %slice-start.2 = ((s8[12582912]{0:T(1024)(128)(4,1)}), s8[4194304]{0:T(1024)(128)(4,1)S(1)}, s32[]{:S(2)}) async-start(s8[12582912]{0:T(1024)(128)(4,1)} %bitcast.213), calls=%async_computation.11 | async-start | bytes 8388608
  259.8 9.9 %copy-start.17 = (bf16[1024,3072]{1,0:T(8,128)(2,1)}, bf16[1024,3072]{1,0:T(8,128)(2,1)S(1)}, u32[]{:S(2)}) copy-start(bf16[1024,3072]{1,0:T(8,128)(2,1)S(1)} %get-tuple-element.286) | copy-start | bytes 18874372
  314.5 9.6 %copy-start.3 = (bf16[4,1024,1024]{1,2,0:T(8,128)(2,1)S(1)}, bf16[4,1024,1024]{1,2,0:T(8,128)(2,1)}, u32[]{:S(2)}) copy-start(bf16[4,1024,1024]{1,2,0:T(8,128)(2,1)} %copy-done.2) | copy-start | bytes 25165828 | tf_op jit(solution)/shard_map/while
  359.7 9.6 %copy-start.3 = (bf16[4,1024,1024]{1,2,0:T(8,128)(2,1)S(1)}, bf16[4,1024,1024]{1,2,0:T(8,128)(2,1)}, u32[]{:S(2)}) copy-start(bf16[4,1024,1024]{1,2,0:T(8,128)(2,1)} %copy-done.2) | copy-start | bytes 25165828 | tf_op jit(solution)/shard_map/while
  404.9 9.7 %copy-start.3 = (bf16[4,1024,1024]{1,2,0:T(8,128)(2,1)S(1)}, bf16[4,1024,1024]{1,2,0:T(8,128)(2,1)}, u32[]{:S(2)}) copy-start(bf16[4,1024,1024]{1,2,0:T(8,128)(2,1)} %copy-done.2) | copy-start | bytes 25165828 | tf_op jit(solution)/shard_map/while
  420.8 8.6 copy-start.43
  434.3 138.2 %all-gather.7.cloned.1.call-start = ((), (), s32[]{:S(2)}) async-start(), calls=%async_computation.4 | async-start | bytes 9437184 | tf_op jit(solution)/shard_map/all_gather | solution.py:294
  444.6 271.0 %reduce-scatter.5.cloned.1.call-start = ((), (), s32[]{:S(2)}) async-start(), calls=%async_computation.6 | async-start | bytes 9732096 | tf_op jit(solution)/shard_map/reduce_scatter | solution.py:285
  454.6 473.2 %reduce-scatter.3.cloned.1.call-start = ((), (), s32[]{:S(2)}) async-start(), calls=%async_computation.5 | async-start | bytes 19464192 | tf_op jit(solution)/shard_map/reduce_scatter | solution.py:282
  572.6 355.2 %copy-start.1 = (bf16[2048,768]{1,0:T(8,128)(2,1)S(1)}, bf16[2048,768]{1,0:T(8,128)(2,1)}, u32[]{:S(2)}) copy-start(bf16[2048,768]{1,0:T(8,128)(2,1)} %param.22) | copy-start | bytes 9437188
  (73 other events, 255.5 us)
Sparse Core Ops, SparseCore 0:
  10.9 84.7 all-gather.8
  98.6 62.1 all-gather.4
  434.5 117.9 all-reduce.2
  553.8 18.6 all-gather.6
  578.9 136.6 reduce-scatter.4
  723.6 204.1 reduce-scatter.2

commit v2 on v1

v2 whole, which is shorter than its diff:
```python
import functools
import math

import jax
import jax.numpy as jnp
from jax import lax
from jax.experimental import pallas as pl
from jax.experimental.pallas import tpu as pltpu
from jax.sharding import PartitionSpec as P

HEAD_DIM = 64
PAIR = 2 * HEAD_DIM
EPS = 1e-05
BLOCK = 256
F32 = jnp.float32
BF16 = jnp.bfloat16
VMEM_LIMIT = 60 * 1024 * 1024


def nn(left, right):
    return lax.dot_general(left, right, (((1,), (0,)), ((), ())), preferred_element_type=F32)


def nt(left, right):
    return lax.dot_general(left, right, (((1,), (1,)), ((), ())), preferred_element_type=F32)


def tn(left, right):
    return lax.dot_general(left, right, (((0,), (0,)), ((), ())), preferred_element_type=F32)


def col_sum(value):
    return jnp.sum(value, axis=0, keepdims=True)


def normalized(value):
    center = jnp.mean(value, axis=-1, keepdims=True)
    centered = value - center
    spread = jnp.mean(centered * centered, axis=-1, keepdims=True)
    scale = lax.rsqrt(spread + EPS)
    return centered * scale, scale


def norm_back(hat, scale, gain, upstream):
    scaled = upstream * gain
    first = jnp.mean(scaled, axis=-1, keepdims=True)
    second = jnp.mean(scaled * hat, axis=-1, keepdims=True)
    return (scaled - first - hat * second) * scale


def params(**more):
    return pltpu.CompilerParams(vmem_limit_bytes=VMEM_LIMIT, **more)


def whole(shape):
    return pl.BlockSpec(shape, lambda *_: (0,) * len(shape))


def project_kernel(x_ref, w_ref, gain_ref, shift_ref, bias_ref, out_ref, normed_ref):
    hat, _ = normalized(x_ref[...].astype(F32))
    normed = (hat * gain_ref[...] + shift_ref[...]).astype(BF16)
    normed_ref[...] = normed
    out_ref[...] = (nn(normed, w_ref[...]) + bias_ref[...]).astype(BF16)


def project(x, weight, gain, shift, bias):
    rows, width = x.shape
    return pl.pallas_call(
        project_kernel,
        grid=(rows // BLOCK,),
        in_specs=[
            pl.BlockSpec((BLOCK, width), lambda i: (i, 0)),
            whole((width, 3 * width)),
            whole((1, width)),
            whole((1, width)),
            whole((1, 3 * width)),
        ],
        out_specs=[
            pl.BlockSpec((BLOCK, 3 * width), lambda i: (i, 0)),
            pl.BlockSpec((BLOCK, width), lambda i: (i, 0)),
        ],
        out_shape=[
            jax.ShapeDtypeStruct((rows, 3 * width), BF16),
            jax.ShapeDtypeStruct((rows, width), BF16),
        ],
        compiler_params=params(),
        name="project",
    )(x, weight, gain, shift, bias)


def allowed_mask(start, key_at, keys, queries):
    key = key_at + lax.broadcasted_iota(jnp.int32, (keys, queries), 0)
    return key >= start


def head_rows(pair_t, head):
    row = lax.broadcasted_iota(jnp.int32, pair_t.shape, 0)
    mine = (row < HEAD_DIM) if head == 0 else (row >= HEAD_DIM)
    return jnp.where(mine, pair_t, jnp.zeros_like(pair_t))


def head_cols(pair, head):
    col = lax.broadcasted_iota(jnp.int32, pair.shape, 1)
    mine = (col < HEAD_DIM) if head == 0 else (col >= HEAD_DIM)
    return jnp.where(mine, pair, jnp.zeros_like(pair))


def masked_scores(key, query_t, start, block):
    keys = (block + 1) * BLOCK
    scores = nn(key[:keys], query_t)
    index = lax.broadcasted_iota(jnp.int32, (keys, BLOCK), 0)
    ok = index >= start
    last = block * BLOCK + lax.broadcasted_iota(jnp.int32, (keys, BLOCK), 1)
    ok = ok & (index <= last)
    return jnp.where(ok, scores, -1e30)


def attend_kernel(q_ref, k_ref, v_ref, start_ref, out_ref, lse_ref):
    rows = q_ref.shape[0]
    query_t = (q_ref[...].astype(F32) * HEAD_DIM**-0.5).T.astype(BF16)
    key = k_ref[...]
    value_t = v_ref[...].astype(F32).T.astype(BF16)
    for block in range(rows // BLOCK):
        at = slice(block * BLOCK, (block + 1) * BLOCK)
        keys = (block + 1) * BLOCK
        start = start_ref[:, at]
        outs = []
        for head in range(2):
            scores = masked_scores(key, head_rows(query_t[:, at], head), start, block)
            peak = jnp.max(scores, axis=0, keepdims=True)
            raised = jnp.exp(scores - peak)
            total = jnp.sum(raised, axis=0, keepdims=True)
            lanes = slice(head * HEAD_DIM, (head + 1) * HEAD_DIM)
            probs = (raised * (1.0 / total)).astype(BF16)
            outs.append(nn(value_t[lanes, :keys], probs))
            lse_ref[0, head : head + 1, at] = peak + jnp.log(total)
        out_ref[at, :] = jnp.concatenate(outs, axis=0).T


def attend(projected, start):
    rows, columns = projected.shape
    width = columns // 3
    pairs = width // PAIR
    return pl.pallas_call(
        attend_kernel,
        grid=(pairs,),
        in_specs=[
            pl.BlockSpec((rows, PAIR), lambda p: (0, p)),
            pl.BlockSpec((rows, PAIR), lambda p: (0, pairs + p)),
            pl.BlockSpec((rows, PAIR), lambda p: (0, 2 * pairs + p)),
            whole((1, rows)),
        ],
        out_specs=[
            pl.BlockSpec((rows, PAIR), lambda p: (0, p)),
            pl.BlockSpec((1, 2, rows), lambda p: (p, 0, 0)),
        ],
        out_shape=[
            jax.ShapeDtypeStruct((rows, width), F32),
            jax.ShapeDtypeStruct((pairs, 2, rows), F32),
        ],
        compiler_params=params(),
        name="attend",
    )(projected, projected, projected, start)


def attend_back_kernel(q_ref, k_ref, v_ref, g_ref, o_ref, lse_ref, start_ref, dq_ref, dk_ref, dv_ref, dk_acc, dv_acc):
    rows = q_ref.shape[0]
    scale = HEAD_DIM**-0.5
    scaled = q_ref[...].astype(F32) * scale
    query = scaled.astype(BF16)
    query_t = scaled.T.astype(BF16)
    key = k_ref[...]
    key_t = key.astype(F32).T.astype(BF16)
    value = v_ref[...]
    grad = g_ref[...]
    grad_f = grad.astype(F32)
    grad_t = grad_f.T.astype(BF16)
    weighted_t = (grad_f * o_ref[...]).T
    dk_acc[...] = jnp.zeros_like(dk_acc)
    dv_acc[...] = jnp.zeros_like(dv_acc)
    for block in range(rows // BLOCK):
        at = slice(block * BLOCK, (block + 1) * BLOCK)
        keys = (block + 1) * BLOCK
        start = start_ref[:, at]
        outs = []
        for head in range(2):
            lanes = slice(head * HEAD_DIM, (head + 1) * HEAD_DIM)
            inner = col_sum(weighted_t[lanes, at])
            scores = masked_scores(key, head_rows(query_t[:, at], head), start, block)
            soft = jnp.exp(scores - lse_ref[0, head : head + 1, at])
            grad_soft = nn(value[:keys], head_rows(grad_t[:, at], head))
            grad_scores = (soft * (grad_soft - inner)).astype(BF16)
            dv_acc[:keys, :] += nn(soft.astype(BF16), head_cols(grad[at], head))
            dk_acc[:keys, :] += nn(grad_scores, head_cols(query[at], head))
            outs.append(nn(key_t[lanes, :keys], grad_scores))
        dq_ref[at, :] = (jnp.concatenate(outs, axis=0) * scale).T.astype(BF16)
    dk_ref[...] = dk_acc[...].astype(BF16)
    dv_ref[...] = dv_acc[...].astype(BF16)


def attend_back(projected, grad_context, context, lse, start):
    rows, columns = projected.shape
    width = columns // 3
    pairs = width // PAIR
    pair = pl.BlockSpec((rows, PAIR), lambda p: (0, p))
    return pl.pallas_call(
        attend_back_kernel,
        grid=(pairs,),
        in_specs=[
            pair,
            pl.BlockSpec((rows, PAIR), lambda p: (0, pairs + p)),
            pl.BlockSpec((rows, PAIR), lambda p: (0, 2 * pairs + p)),
            pair,
            pair,
            pl.BlockSpec((1, 2, rows), lambda p: (p, 0, 0)),
            whole((1, rows)),
        ],
        out_specs=[pair] * 3,
        out_shape=[jax.ShapeDtypeStruct((rows, width), BF16)] * 3,
        scratch_shapes=[pltpu.VMEM((rows, PAIR), F32), pltpu.VMEM((rows, PAIR), F32)],
        compiler_params=params(),
        name="attend_back",
    )(projected, projected, projected, grad_context, context, lse, start)


def gelu_parts(value):
    phi = 0.5 * (1.0 + lax.erf(value * (1.0 / math.sqrt(2.0))))
    bell = jnp.exp(-0.5 * value * value) * (1.0 / math.sqrt(2.0 * math.pi))
    return value * phi, phi + value * bell


def middle_kernel(
    x_ref, dy_ref, ctx_ref, alive_ref, wo_ref, wu_ref, wd_ref,
    sg_ref, ss_ref, ob_ref, fg_ref, fs_ref, ub_ref, mg_ref, ms_ref, db_ref,
    out_ref, ghid_ref, gctx_ref, mixed_ref, gbranch_ref, nffn_ref, gup_ref, mid_ref, gffn_ref,
    narrow_ref, wide_ref,
):
    step = pl.program_id(0)

    @pl.when(step == 0)
    def _():
        narrow_ref[...] = jnp.zeros_like(narrow_ref)
        wide_ref[...] = jnp.zeros_like(wide_ref)

    alive = alive_ref[...]
    ctx_hat, ctx_scale = normalized(ctx_ref[...])
    mixed = (ctx_hat * sg_ref[...] + ss_ref[...]).astype(BF16)
    mixed_ref[...] = mixed
    branch = nn(mixed, wo_ref[...]) + ob_ref[...]
    hidden = (x_ref[...].astype(F32) + alive * branch).astype(BF16).astype(F32)
    hid_hat, hid_scale = normalized(hidden)
    nffn = (hid_hat * fg_ref[...] + fs_ref[...]).astype(BF16)
    nffn_ref[...] = nffn
    upper = nn(nffn, wu_ref[...]) + ub_ref[...]
    active, slope = gelu_parts(upper)
    act_hat, act_scale = normalized(active)
    mid = (act_hat * mg_ref[...] + ms_ref[...]).astype(BF16)
    mid_ref[...] = mid
    result = (nn(mid, wd_ref[...]) + db_ref[...]).astype(BF16).astype(F32)
    out_ref[...] = hidden + alive * result

    upstream = dy_ref[...].astype(F32)
    gffn = (alive * upstream).astype(BF16)
    gffn_ref[...] = gffn
    gmid = nt(gffn, wd_ref[...])
    gact = norm_back(act_hat, act_scale, mg_ref[...], gmid)
    gup = (gact * slope).astype(BF16)
    gup_ref[...] = gup
    wide_ref[0:1, :] += col_sum(gup.astype(F32))
    wide_ref[1:2, :] += col_sum(gmid * act_hat)
    wide_ref[2:3, :] += col_sum(gmid)
    gnffn = nt(gup, wu_ref[...])
    ghid = (upstream + norm_back(hid_hat, hid_scale, fg_ref[...], gnffn)).astype(BF16)
    ghid_ref[...] = ghid
    gbranch = (alive * ghid.astype(F32)).astype(BF16)
    gbranch_ref[...] = gbranch
    gmixed = nt(gbranch, wo_ref[...])
    gctx_ref[...] = norm_back(ctx_hat, ctx_scale, sg_ref[...], gmixed).astype(BF16)
    narrow_ref[0:1, :] += col_sum(gmixed * ctx_hat)
    narrow_ref[1:2, :] += col_sum(gmixed)
    narrow_ref[2:3, :] += col_sum(gbranch.astype(F32))
    narrow_ref[3:4, :] += col_sum(gnffn * hid_hat)
    narrow_ref[4:5, :] += col_sum(gnffn)
    narrow_ref[5:6, :] += col_sum(gffn.astype(F32))


def middle(x, dy, context, alive, attention_block, up_weight, down_weight, vectors):
    rows, width = x.shape
    hidden = up_weight.shape[1]
    row = pl.BlockSpec((BLOCK, width), lambda i: (i, 0))
    row_wide = pl.BlockSpec((BLOCK, hidden), lambda i: (i, 0))
    once = dict(pipeline_mode=pl.Buffered(1))
    narrow = whole((1, width))
    wide = whole((1, hidden))
    def shape(columns, dtype):
        return jax.ShapeDtypeStruct((rows, columns), dtype)
    return pl.pallas_call(
        middle_kernel,
        grid=(rows // BLOCK,),
        in_specs=[
            row, row, row,
            pl.BlockSpec((BLOCK, 1), lambda i: (i, 0)),
            pl.BlockSpec((width, width), lambda i: (0, 3), **once),
            pl.BlockSpec((width, hidden), lambda i: (0, 0), **once),
            pl.BlockSpec((hidden, width), lambda i: (0, 0), **once),
            narrow, narrow, narrow, narrow, narrow, wide, wide, wide, narrow,
        ],
        out_specs=[row, row, row, row, row, row, row_wide, row_wide, row, whole((8, width)), whole((8, hidden))],
        out_shape=[
            shape(width, F32), shape(width, BF16), shape(width, BF16), shape(width, BF16), shape(width, BF16),
            shape(width, BF16), shape(hidden, BF16), shape(hidden, BF16), shape(width, BF16),
            jax.ShapeDtypeStruct((8, width), F32), jax.ShapeDtypeStruct((8, hidden), F32),
        ],
        compiler_params=params(),
        name="middle",
    )(x, dy, context, alive, attention_block, up_weight, down_weight, *vectors)


def outer_kernel(left_ref, right_ref, out_ref):
    out_ref[...] = tn(left_ref[...], right_ref[...]).astype(out_ref.dtype)


def outer(left, right, tile, dtype, name):
    rows, across = left.shape
    columns = right.shape[1]
    return pl.pallas_call(
        outer_kernel,
        grid=(across // tile,),
        in_specs=[pl.BlockSpec((rows, tile), lambda i: (0, i)), whole((rows, columns))],
        out_specs=pl.BlockSpec((tile, columns), lambda i: (i, 0)),
        out_shape=jax.ShapeDtypeStruct((across, columns), dtype),
        compiler_params=params(),
        name=name,
    )(left, right)


def project_back_kernel(dq_ref, dk_ref, dv_ref, w_ref, x_ref, ghid_ref, gain_ref, out_ref, narrow_ref):
    step = pl.program_id(0)
    width = x_ref.shape[1]

    @pl.when(step == 0)
    def _():
        narrow_ref[...] = jnp.zeros_like(narrow_ref)

    dq, dk, dv = dq_ref[...], dk_ref[...], dv_ref[...]
    gnormed = nt(dq, w_ref[:, :width]) + nt(dk, w_ref[:, width : 2 * width]) + nt(dv, w_ref[:, 2 * width :])
    hat, scale = normalized(x_ref[...].astype(F32))
    out_ref[...] = ghid_ref[...].astype(F32) + norm_back(hat, scale, gain_ref[...], gnormed)
    narrow_ref[0:1, :] += col_sum(gnormed * hat)
    narrow_ref[1:2, :] += col_sum(gnormed)
    narrow_ref[2:3, :] += col_sum(dq.astype(F32))
    narrow_ref[3:4, :] += col_sum(dv.astype(F32))


def project_back(dq, dk, dv, weight, x, ghid, gain):
    rows, width = x.shape
    row = pl.BlockSpec((BLOCK, width), lambda i: (i, 0))
    return pl.pallas_call(
        project_back_kernel,
        grid=(rows // BLOCK,),
        in_specs=[row, row, row, whole((width, 3 * width)), row, row, whole((1, width))],
        out_specs=[row, whole((8, width))],
        out_shape=[jax.ShapeDtypeStruct((rows, width), F32), jax.ShapeDtypeStruct((8, width), F32)],
        compiler_params=params(),
        name="project_back",
    )(dq, dk, dv, weight, x, ghid, gain)


def row_marks(lengths_row, count):
    slots = jnp.arange(lengths_row.shape[0], dtype=jnp.int32)
    ends = jnp.sum(jnp.where(slots[:, None] <= slots[None, :], lengths_row[:, None], 0), axis=0)
    index = jnp.arange(count, dtype=jnp.int32)
    before = jnp.where(ends[None, :] <= index[:, None], ends[None, :], 0)
    alive = index < jnp.max(ends)
    start = jnp.where(alive, jnp.max(before, axis=1), index)
    return alive.astype(F32)[:, None], start[None, :]


def one_batch(x, dy, lengths_row, attention_block, up_weight, down_weight, vectors):
    (pre_gain, pre_shift, query_bias, value_bias, sub_gain, sub_shift, out_bias,
     ffn_gain, ffn_shift, up_bias, mid_gain, mid_shift, down_bias) = [v[None, :] for v in vectors]
    count, width = x.shape
    alive, start = row_marks(lengths_row, count)
    bias = jnp.concatenate([query_bias, jnp.zeros_like(query_bias), value_bias], axis=1)
    projected, normed = project(x, attention_block, pre_gain, pre_shift, bias)
    context, lse = attend(projected, start)
    out, ghid, gctx, mixed, gbranch, nffn, gup, mid, gffn, narrow, wide = middle(
        x, dy, context, alive, attention_block, up_weight, down_weight,
        (sub_gain, sub_shift, out_bias, ffn_gain, ffn_shift, up_bias, mid_gain, mid_shift, down_bias),
    )
    grad_up = outer(nffn, gup, 256, F32, "outer_up")
    grad_down = outer(mid, gffn, 512, F32, "outer_down")
    dq, dk, dv = attend_back(projected, gctx, context, lse, start)
    grad_out = outer(mixed, gbranch, 256, F32, "outer_out")
    grad_x, pre = project_back(dq, dk, dv, attention_block, x, ghid, pre_gain)
    grads = [outer(normed, d, 256, F32, "outer_qkv") for d in (dq, dk, dv)]
    grad_attention = jnp.concatenate(grads + [grad_out], axis=1)
    small = (pre[0], pre[1], pre[2], pre[3], narrow[0], narrow[1], narrow[2], narrow[3], narrow[4],
             wide[0], wide[1], wide[2], narrow[5])
    return (out, grad_x), (grad_attention, grad_up, grad_down, small)


def shards(tokens, out_grad, seq_lengths, half_weights, down_weight, *all_vectors):
    section = lax.axis_index("section")
    sections = lax.axis_size("section")
    both = ("section", "dp")
    width = tokens.shape[1]
    batches = seq_lengths.shape[0]
    count = tokens.shape[0] // batches
    own_batches = batches // sections
    own_rows = own_batches * count
    hidden_units = half_weights.shape[2]
    shares = sections * lax.axis_size("dp")

    blocks = lax.all_gather(half_weights[0], both, axis=0, tiled=True)
    blocks = blocks.reshape(sections, width, hidden_units)
    down_full = lax.all_gather(down_weight, both, axis=0, tiled=True)

    def own(array, rows):
        return lax.dynamic_slice_in_dim(array, section * rows, rows, axis=0)

    x_rows = own(tokens, own_rows)
    dy_rows = own(out_grad, own_rows)
    lengths = own(seq_lengths, own_batches)
    rows, sums = [], None
    for index in range(own_batches):
        at = slice(index * count, (index + 1) * count)
        row, more = one_batch(x_rows[at], dy_rows[at], lengths[index], blocks[0], blocks[1], down_full, all_vectors)
        rows.append(row)
        sums = more if sums is None else jax.tree.map(jnp.add, sums, more)
    out_block = jnp.concatenate([row[0] for row in rows], axis=0)
    grad_rows = jnp.concatenate([row[1] for row in rows], axis=0)
    grad_attention, grad_up, grad_down, vectors = sums

    block_part = lax.psum_scatter(
        jnp.concatenate([grad_attention, grad_up], axis=0), both, scatter_dimension=0, tiled=True
    )
    down_part = lax.psum_scatter(grad_down, both, scatter_dimension=0, tiled=True)
    packed = jnp.concatenate([vector.reshape(shares, -1) for vector in vectors], axis=1)
    packed = lax.psum_scatter(packed, both, scatter_dimension=0, tiled=True).reshape(-1)
    parts, start = [], 0
    for vector in vectors:
        size = vector.shape[0] // shares
        parts.append(packed[start : start + size])
        start += size

    layer_out = lax.all_gather(out_block, "section", axis=0, tiled=True)
    tokens_grad = lax.all_to_all(grad_rows, "section", split_axis=1, concat_axis=0, tiled=True)
    return (layer_out, tokens_grad, block_part[None], down_part, *parts)


def solution(mesh):
    replicated = P()
    return jax.shard_map(
        shards,
        mesh=mesh,
        in_specs=(P("dp", None), P("dp", None), P("dp", None), P("section", "dp", None), P(("section", "dp"), None))
        + (replicated,) * 13,
        out_specs=(P("dp", None), P("dp", "section"), P("section", "dp", None), P(("section", "dp"), None))
        + (P(("section", "dp")),) * 13,
        check_vma=False,
    )
```

time: 940 us -> 756 us (0.80)
  matrix products: 233 us -> 0 us
  Pallas kernels: 0 us -> 163 us
  other arithmetic: 106 us -> 20 us
  local copies, waits for them, and re-layouts: 68.8 us -> 40.1 us
    dot_general x33 -> x0, matrix products: 233 us -> none  [the longest x4 46.4 us: contract_cols(): lax.dot_general(left, right, (((1,), (1,)), ((), ())), preferred_element_...]
    pallas_call x0 -> x11, Pallas kernels: none -> 163 us  [the longest x1 46.2 us: middle(): pl.pallas_call(middle_kernel, grid=(rows // BLOCK,), in_specs=[row, row,...]
    reduce_sum x17 -> x1, other arithmetic: 53.3 us -> 0.08 us  [row_marks(): jnp.sum(jnp.where(slots[:, None] <= slots[None, :], lengths_row[:, None],...]
    convert_element_type x6 -> x1, other arithmetic: 25.5 us -> 1.5 us  [row_marks(): return (alive.astype(F32)[:, None], start[None, :])]
    dynamic_slice x18 -> x0, local copies, waits for them, and re-layouts: 20.5 us -> none  [attention_forward(): context, logsum = lax.map(one_group, (query, key, value))]
    all_gather x1, waiting for transfers between devices: 0.01 us -> 17.2 us  [shards(): down_full = lax.all_gather(down_weight, both, axis=0, tiled=True)]
    and x6 -> x0, other arithmetic: 13.8 us -> none  [row_masks(): same & causal & (alive[:, None] | (index[:, None] == index[None, :]))]
    broadcast_in_dim x2 -> x12, local copies, waits for them, and re-layouts: 0.01 us -> 11.6 us  [the longest x10 11.5 us: one_batch(): v[None, :]]
  transfers between devices with their start and end apart: 6 -> 6, of which waited for: 5 -> 6; matrix products, arithmetic and copies ran while one was open for 19% -> 6% of each run, Pallas kernels for 0% -> 11%
where the time goes in v2:
time: 756 us; the launch traced here: 755 us
  waiting for transfers between devices  511 us (68%)
  Pallas kernels  163 us (22%)
  local copies, waits for them, and re-layouts  40.1 us (5%)
  other arithmetic  20 us (3%)
  between operations  14.3 us (2%)
    reduce_scatter x1, waiting for transfers between devices, shards(): lax.psum_scatter(jnp.concatenate([grad_attention, grad_up], axis=0), both...  212 us
    reduce_scatter x1, waiting for transfers between devices, shards(): lax.psum_scatter(grad_down, both, scatter_dimension=0, tiled=True)  143 us
    all_gather x1, waiting for transfers between devices, shards(): blocks = lax.all_gather(half_weights[0], both, axis=0, tiled=True)  67.5 us
    unnamed x7, waiting for transfers between devices  54.1 us
    pallas_call x1, Pallas kernels, middle(): pl.pallas_call(middle_kernel, grid=(rows // BLOCK,), in_specs=[row, row,...  46.2 us
    pallas_call x6, Pallas kernels, outer(): pl.pallas_call(outer_kernel, grid=(across // tile,), in_specs=[pl.BlockSp...  41.4 us
    pallas_call x1, Pallas kernels, attend(): pl.pallas_call(attend_kernel, grid=(pairs,), in_specs=[pl.BlockSpec((rows...  31.1 us
    pallas_call x1, Pallas kernels, attend_back(): pl.pallas_call(attend_back_kernel, grid=(pairs,), in_specs=[pair, pl.Bloc...  25.6 us
  transfers between devices with their start and end apart: 6, of which 6 were waited for; matrix products, arithmetic and copies ran while one was open for 6% of the time, Pallas kernels for 11%

profile of v2, /device:TPU:0, one launch (start us, length us, event | category | flops | bytes accessed | tf_op | source)
XLA Modules:
  0.0 754.8 jit_solution(13229194642517909017)
XLA Ops:
  22.6 3.8 constant_dynamic-slice_fusion.1
  28.2 67.5 %all-gather.9.cloned.1.call-done = bf16[1,1536,3072]{2,1,0:T(8,128)(2,1)} async-done(((bf16[1,48,3072]{2,1,0:T(8,128)(2,1)}), bf16[1,1536,3072]{2,1,0:T(8,128)(2,1)}) %all-gather.9.cloned.1.call-update) | async-done | bytes 9437200 | tf_op jit(solution)/shard_map/all_gather | solution.py:415
  95.7 8.3 %slice_bitcast_fusion = (bf16[768,3072]{1,0:T(8,128)(2,1)}, bf16[768,3072]{1,0:T(8,128)(2,1)}) fusion(bf16[1,1536,3072]{2,1,0:T(8,128)(2,1)} %all-gather.9.cloned.1.call-done), kind=kLoop, calls=%fused_computation.1 | loop fusion | bytes 18874368 | tf_op jit(solution)/shard_map/slice | solution.py:428
  104.0 8.6 %project.1 = (bf16[1024,2304]{1,0:T(8,128)(2,1)}, bf16[1024,768]{1,0:T(8,128)(2,1)}) custom-call(bf16[1024,768]{1,0:T(8,128)(2,1)} %get-tuple-element.86.x_ref, bf16[768,3072]{1,0:T(8,128)(2,1)} %get-tuple-element.71.w_ref.wo_ref, f32[1,768]{1,0:T(1,128)} %broadcast_in_dim.76.gain_ref, f32[1,768]{1,0:T(1,128)} %broadcast_in_dim.77.shift_ref, ...), custom_call_target="tpu_custom_call" | custom-call | tf_op jit(solution)/shard_map/project/pallas_call | solution.py:68
  112.5 31.1 %attend.1 = (f32[1024,768]{1,0:T(8,128)}, f32[6,2,1024]{2,1,0:T(2,128)}) custom-call(bf16[1024,2304]{1,0:T(8,128)(2,1)} %get-tuple-element.37.q_ref.k_ref.v_ref, bf16[1024,2304]{1,0:T(8,128)(2,1)} %get-tuple-element.37.q_ref.k_ref.v_ref, bf16[1024,2304]{1,0:T(8,128)(2,1)} %get-tuple-element.37.q_ref.k_ref.v_ref, s32[1,1024]{1,0:T(1,128)} %compare_select_fusion.start_ref), custom_call_target="tpu_custom_call" | custom-call | tf_op jit(solution)/shard_map/attend/pallas_call | solution.py:144
  143.6 17.2 %all-gather.5.cloned.1.call-done.wd_ref = bf16[3072,768]{1,0:T(8,128)(2,1)} async-done(((bf16[96,768]{1,0:T(8,128)(2,1)}), bf16[3072,768]{1,0:T(8,128)(2,1)}) %all-gather.5.cloned.1.call-update) | async-done | bytes 4718608 | tf_op jit(solution)/shard_map/all_gather | solution.py:417
  160.8 46.2 %middle.1 = (f32[1024,768]{1,0:T(8,128)}, bf16[1024,768]{1,0:T(8,128)(2,1)}, bf16[1024,768]{1,0:T(8,128)(2,1)}, bf16[1024,768]{1,0:T(8,128)(2,1)}, bf16[1024,768...) custom-call(bf16[1024,768]{1,0:T(8,128)(2,1)} %get-tuple-element.86., ...), custom_call_target="tpu_custom_call" | custom-call | tf_op jit(solution)/shard_map/middle/pallas_call | solution.py:297
  207.1 25.6 %attend_back.1 = (bf16[1024,768]{1,0:T(8,128)(2,1)}, bf16[1024,768]{1,0:T(8,128)(2,1)}, bf16[1024,768]{1,0:T(8,128)(2,1)}) custom-call(bf16[1024,2304]{1,0:T(8,128)(2,1)} %get-tuple-element.37.q_ref.k_ref.v_ref, bf16[1024,2304]{1,0:T(8,128)(2,1)} %get-tuple-element.37.q_ref.k_ref.v_ref, bf16[1024,2304]{1,0:T(8,128)(2,1)} %get-tuple-element.37.q_ref.k_ref.v_ref, ...), custom_call_target="tpu_custom_call" | custom-call | tf_op jit(solution)/shard_map/attend_back/pallas_call | solution.py:206
  232.7 9.9 %project_back.1 = (f32[1024,768]{1,0:T(8,128)}, f32[8,768]{1,0:T(8,128)}) custom-call(bf16[1024,768]{1,0:T(8,128)(2,1)} %get-tuple-element.42.dq_ref.right_ref, bf16[1024,768]{1,0:T(8,128)(2,1)} %get-tuple-element.43.dk_ref.right_ref, bf16[1024,768]{1,0:T(8,128)(2,1)} %get-tuple-element.44.dv_ref.right_ref, ...), custom_call_target="tpu_custom_call" | custom-call | tf_op jit(solution)/shard_map/project_back/pallas_call | solution.py:358
  247.2 10.8 %outer_down.1 = f32[3072,768]{1,0:T(8,128)} custom-call(bf16[1024,3072]{1,0:T(8,128)(2,1)} %get-tuple-element.52.left_ref, bf16[1024,768]{1,0:T(8,128)(2,1)} %get-tuple-element.53.right_ref), custom_call_target="tpu_custom_call" | custom-call | tf_op jit(solution)/shard_map/outer_down/pallas_call | solution.py:326
  258.0 5.1 outer_qkv.3
  263.1 5.1 outer_qkv.4
  268.2 5.1 outer_qkv.5
  273.2 5.1 outer_out.1
  278.3 10.3 %outer_up.1 = f32[768,3072]{1,0:T(8,128)} custom-call(bf16[1024,768]{1,0:T(8,128)(2,1)} %get-tuple-element.50.left_ref, bf16[1024,3072]{1,0:T(8,128)(2,1)} %get-tuple-element.51.right_ref), custom_call_target="tpu_custom_call" | custom-call | tf_op jit(solution)/shard_map/outer_up/pallas_call | solution.py:326
  288.7 15.8 %pad_maximum_fusion = f32[1536,3072]{1,0:T(8,128)} fusion(f32[768,3072]{1,0:T(8,128)} %outer_up.1, f32[768,768]{1,0:T(8,128)} %outer_out.1, f32[768,768]{1,0:T(8,128)} %outer_qkv.5, f32[768,768]{1,0:T(8,128)} %outer_qkv.4, f32[768,768]{1,0:T(8,128)S(1)} %copy-done.2), kind=kLoop, calls=%fused_computation | loop fusion | flops 18874368 | bytes 37748736 | tf_op jit(solution)/shard_map/concatenate | solution.py:436
  304.5 1.9 copy-done.3
  306.6 6.3 all_to_all.19
  312.8 52.1 %all-reduce.3.cloned.1.call-done = f32[32,528]{1,0:T(8,128)} async-done(((f32[32,528]{1,0:T(8,128)}), f32[32,528]{1,0:T(8,128)}) %all-reduce.3.cloned.1.call-update) | async-done | bytes 67600
  368.0 17.1 %all-gather.7.cloned.1.call-done = f32[2048,768]{1,0:T(8,128)} async-done(((f32[1024,768]{1,0:T(8,128)}), f32[2048,768]{1,0:T(8,128)}) %all-gather.7.cloned.1.call-update) | async-done | bytes 6291472 | tf_op jit(solution)/shard_map/all_gather | solution.py:447
  385.1 143.0 %reduce-scatter.5.cloned.1.call-done = f32[96,768]{1,0:T(8,128)} async-done(((f32[3072,768]{1,0:T(8,128)}), f32[96,768]{1,0:T(8,128)}) %reduce-scatter.5.cloned.1.call-update) | async-done | bytes 294928 | tf_op jit(solution)/shard_map/reduce_scatter | solution.py:438
  528.2 212.2 %reduce-scatter.3.cloned.1.call-done = f32[48,3072]{1,0:T(8,128)} async-done(((f32[1536,3072]{1,0:T(8,128)}), f32[48,3072]{1,0:T(8,128)}) %reduce-scatter.3.cloned.1.call-update) | async-done | bytes 589840 | tf_op jit(solution)/shard_map/reduce_scatter | solution.py:435
  740.4 5.9 copy.45
  746.3 1.7 copy.46
  (60 shorter events, 25.0 us)
Async XLA Ops:
  7.2 13.1 %copy-start = (s32[2,8]{1,0:T(2,128)S(1)}, s32[2,8]{1,0:T(2,128)}, u32[]{:S(2)}) copy-start(s32[2,8]{1,0:T(2,128)} %param.20) | copy-start | bytes 196
  7.2 88.5 %all-gather.9.cloned.1.call-start = ((), (), s32[]{:S(2)}) async-start(), calls=%async_computation.7 | async-start | bytes 9732096 | tf_op jit(solution)/shard_map/all_gather | solution.py:415
  7.9 152.9 %all-gather.5.cloned.1.call-start = ((), (), s32[]{:S(2)}) async-start(), calls=%async_computation.3 | async-start | bytes 4866048 | tf_op jit(solution)/shard_map/all_gather | solution.py:417
  8.7 356.3 %all-reduce.3.cloned.1.call-start = ((), (), s32[]{:S(2)}) async-start(), calls=%async_computation.8 | async-start | bytes 163840
  232.7 11.1 %copy-start.4 = (f32[8,768]{1,0:T(8,128)S(1)}, f32[8,768]{1,0:T(8,128)}, u32[]{:S(2)}) copy-start(f32[8,768]{1,0:T(8,128)} %get-tuple-element.55) | copy-start | bytes 73732
  246.5 138.6 %all-gather.7.cloned.1.call-start = ((), (), s32[]{:S(2)}) async-start(), calls=%async_computation.4 | async-start | bytes 9437184 | tf_op jit(solution)/shard_map/all_gather | solution.py:447
  247.1 281.0 %reduce-scatter.5.cloned.1.call-start = ((), (), s32[]{:S(2)}) async-start(), calls=%async_computation.6 | async-start | bytes 9732096 | tf_op jit(solution)/shard_map/reduce_scatter | solution.py:438
  258.0 482.4 %reduce-scatter.3.cloned.1.call-start = ((), (), s32[]{:S(2)}) async-start(), calls=%async_computation.5 | async-start | bytes 19464192 | tf_op jit(solution)/shard_map/reduce_scatter | solution.py:435
  278.3 10.3 %copy-start.2 = (f32[768,768]{1,0:T(8,128)S(1)}, f32[768,768]{1,0:T(8,128)}, u32[]{:S(2)}) copy-start(f32[768,768]{1,0:T(8,128)} %outer_qkv.3) | copy-start | bytes 7077892
  304.5 1.9 copy-start.3
  740.4 7.6 %copy-start.1 = (s32[2,8]{1,0:T(2,128)S(1)}, s32[2,8]{1,0:T(2,128)}, u32[]{:S(2)}) copy-start(s32[2,8]{1,0:T(2,128)} %param.20) | copy-start | bytes 196
Sparse Core Ops, SparseCore 0:
  10.9 84.7 all-gather.8
  98.6 62.1 all-gather.4
  246.7 118.2 all-reduce.2
  366.4 18.6 all-gather.6
  391.4 136.6 reduce-scatter.4
  536.1 204.1 reduce-scatter.2

commit v3 on v2

--- a/solution.py
+++ b/solution.py
@@ -50,6 +50,14 @@
 
 def params(**more):
     return pltpu.CompilerParams(vmem_limit_bytes=VMEM_LIMIT, **more)
+
+
+def side_by_side(ref):
+    return jnp.concatenate([ref[b] for b in range(6)], axis=1)
+
+
+def stacked(ref):
+    return jnp.concatenate([jnp.concatenate([ref[3 * h + k] for k in range(3)], axis=1) for h in range(2)], axis=0)
 
 
 def whole(shape):
@@ -242,39 +250,42 @@
         narrow_ref[...] = jnp.zeros_like(narrow_ref)
         wide_ref[...] = jnp.zeros_like(wide_ref)
 
+    out_weight = side_by_side(wo_ref)
+    up_weight = side_by_side(wu_ref)
+    down_weight = stacked(wd_ref)
     alive = alive_ref[...]
     ctx_hat, ctx_scale = normalized(ctx_ref[...])
     mixed = (ctx_hat * sg_ref[...] + ss_ref[...]).astype(BF16)
     mixed_ref[...] = mixed
-    branch = nn(mixed, wo_ref[...]) + ob_ref[...]
+    branch = nn(mixed, out_weight) + ob_ref[...]
     hidden = (x_ref[...].astype(F32) + alive * branch).astype(BF16).astype(F32)
     hid_hat, hid_scale = normalized(hidden)
     nffn = (hid_hat * fg_ref[...] + fs_ref[...]).astype(BF16)
     nffn_ref[...] = nffn
-    upper = nn(nffn, wu_ref[...]) + ub_ref[...]
+    upper = nn(nffn, up_weight) + ub_ref[...]
     active, slope = gelu_parts(upper)
     act_hat, act_scale = normalized(active)
     mid = (act_hat * mg_ref[...] + ms_ref[...]).astype(BF16)
     mid_ref[...] = mid
-    result = (nn(mid, wd_ref[...]) + db_ref[...]).astype(BF16).astype(F32)
+    result = (nn(mid, down_weight) + db_ref[...]).astype(BF16).astype(F32)
     out_ref[...] = hidden + alive * result
 
     upstream = dy_ref[...].astype(F32)
     gffn = (alive * upstream).astype(BF16)
     gffn_ref[...] = gffn
-    gmid = nt(gffn, wd_ref[...])
+    gmid = nt(gffn, down_weight)
     gact = norm_back(act_hat, act_scale, mg_ref[...], gmid)
     gup = (gact * slope).astype(BF16)
     gup_ref[...] = gup
     wide_ref[0:1, :] += col_sum(gup.astype(F32))
     wide_ref[1:2, :] += col_sum(gmid * act_hat)
     wide_ref[2:3, :] += col_sum(gmid)
-    gnffn = nt(gup, wu_ref[...])
+    gnffn = nt(gup, up_weight)
     ghid = (upstream + norm_back(hid_hat, hid_scale, fg_ref[...], gnffn)).astype(BF16)
     ghid_ref[...] = ghid
     gbranch = (alive * ghid.astype(F32)).astype(BF16)
     gbranch_ref[...] = gbranch
-    gmixed = nt(gbranch, wo_ref[...])
+    gmixed = nt(gbranch, out_weight)
     gctx_ref[...] = norm_back(ctx_hat, ctx_scale, sg_ref[...], gmixed).astype(BF16)
     narrow_ref[0:1, :] += col_sum(gmixed * ctx_hat)
     narrow_ref[1:2, :] += col_sum(gmixed)
@@ -284,9 +295,9 @@
     narrow_ref[5:6, :] += col_sum(gffn.astype(F32))
 
 
-def middle(x, dy, context, alive, attention_block, up_weight, down_weight, vectors):
+def middle(x, dy, context, alive, out_weight, up_weight, down_weight, vectors):
     rows, width = x.shape
-    hidden = up_weight.shape[1]
+    hidden = 6 * up_weight.shape[2]
     row = pl.BlockSpec((BLOCK, width), lambda i: (i, 0))
     row_wide = pl.BlockSpec((BLOCK, hidden), lambda i: (i, 0))
     once = dict(pipeline_mode=pl.Buffered(1))
@@ -300,9 +311,9 @@
         in_specs=[
             row, row, row,
             pl.BlockSpec((BLOCK, 1), lambda i: (i, 0)),
-            pl.BlockSpec((width, width), lambda i: (0, 3), **once),
-            pl.BlockSpec((width, hidden), lambda i: (0, 0), **once),
-            pl.BlockSpec((hidden, width), lambda i: (0, 0), **once),
+            pl.BlockSpec(out_weight.shape, lambda i: (0, 0, 0), **once),
+            pl.BlockSpec(up_weight.shape, lambda i: (0, 0, 0), **once),
+            pl.BlockSpec(down_weight.shape, lambda i: (0, 0, 0), **once),
             narrow, narrow, narrow, narrow, narrow, wide, wide, wide, narrow,
         ],
         out_specs=[row, row, row, row, row, row, row_wide, row_wide, row, whole((8, width)), whole((8, hidden))],
@@ -313,7 +324,7 @@
         ],
         compiler_params=params(),
         name="middle",
-    )(x, dy, context, alive, attention_block, up_weight, down_weight, *vectors)
+    )(x, dy, context, alive, out_weight, up_weight, down_weight, *vectors)
 
 
 def outer_kernel(left_ref, right_ref, out_ref):
@@ -343,7 +354,9 @@
         narrow_ref[...] = jnp.zeros_like(narrow_ref)
 
     dq, dk, dv = dq_ref[...], dk_ref[...], dv_ref[...]
-    gnormed = nt(dq, w_ref[:, :width]) + nt(dk, w_ref[:, width : 2 * width]) + nt(dv, w_ref[:, 2 * width :])
+    gnormed = sum(
+        nt(d, jnp.concatenate([w_ref[2 * n], w_ref[2 * n + 1]], axis=1)) for n, d in enumerate((dq, dk, dv))
+    )
     hat, scale = normalized(x_ref[...].astype(F32))
     out_ref[...] = ghid_ref[...].astype(F32) + norm_back(hat, scale, gain_ref[...], gnormed)
     narrow_ref[0:1, :] += col_sum(gnormed * hat)
@@ -358,7 +371,7 @@
     return pl.pallas_call(
         project_back_kernel,
         grid=(rows // BLOCK,),
-        in_specs=[row, row, row, whole((width, 3 * width)), row, row, whole((1, width))],
+        in_specs=[row, row, row, whole(weight.shape), row, row, whole((1, width))],
         out_specs=[row, whole((8, width))],
         out_shape=[jax.ShapeDtypeStruct((rows, width), F32), jax.ShapeDtypeStruct((8, width), F32)],
         compiler_params=params(),
@@ -376,23 +389,294 @@
     return alive.astype(F32)[:, None], start[None, :]
 
 
-def one_batch(x, dy, lengths_row, attention_block, up_weight, down_weight, vectors):
+MESH = pl.DeviceIdType.MESH
+BITS = 4
+CHAINS = ((3, 2, 1, 0), (0, 3, 2, 1), (1, 0, 3, 2))
+
+
+def place():
+    core = lax.axis_index("section")
+    chip = lax.axis_index("dp")
+    return core, chip, [(chip // (1 << bit)) % 2 for bit in range(BITS)]
+
+
+def partner_of(chip, bits, bit):
+    return chip + (1 - 2 * bits[bit]) * (1 << bit)
+
+
+def at_bits(ref, values):
+    return ref.at[tuple(values[bit] for bit in reversed(range(BITS)))]
+
+
+def remote(source, target, sems, device):
+    return pltpu.make_async_remote_copy(
+        src_ref=source, dst_ref=target, send_sem=sems[0], recv_sem=sems[1], device_id=device, device_id_type=MESH
+    )
+
+
+class Gather:
+    def __init__(self, own, other, order, sems, pass_sems):
+        self.own, self.other, self.order = own, other, order
+        self.sems, self.pass_sems = sems, pass_sems
+        self.core, self.chip, self.bits = place()
+
+    def step(self, stage):
+        done = self.order[:stage]
+        values = [slice(None) if bit in done else self.bits[bit] for bit in range(BITS)]
+        part = at_bits(self.own, values)
+        device = (self.core, partner_of(self.chip, self.bits, self.order[stage]))
+        return remote(part, part, (self.sems.at[0, stage], self.sems.at[1, stage]), device)
+
+    def onward(self, stage, ref):
+        done = self.order[:stage]
+        values = [slice(None) if bit in done else self.bits[bit] for bit in range(BITS)]
+        values[self.order[stage]] = 1 - self.bits[self.order[stage]]
+        part = at_bits(ref, values)
+        return remote(part, part, (self.pass_sems.at[0, stage], self.pass_sems.at[1, stage]), (1 - self.core, self.chip))
+
+    def arrive(self, stage):
+        self.step(stage).wait_recv()
+        if stage + 1 < BITS:
+            self.step(stage + 1).start()
+        self.onward(stage, self.own).start()
+
+    def passed(self, stage):
+        self.onward(stage, self.other).wait_recv()
+
+    def drain(self):
+        for stage in range(BITS):
+            self.step(stage).wait_send()
+            self.onward(stage, self.own).wait_send()
+
+
+def greet():
+    core, chip, bits = place()
+    barrier = pltpu.get_barrier_semaphore()
+    others = [(1 - core, chip)] + [(core, partner_of(chip, bits, bit)) for bit in range(BITS)]
+    for other in others:
+        pl.semaphore_signal(barrier, inc=1, device_id=other, device_id_type=MESH)
+    pl.semaphore_wait(barrier, len(others))
+
+
+def seed(parts, full, me, sems, sender):
+    core, chip, bits = place()
+    moves = []
+    for index, (source, block) in enumerate(parts):
+        here = at_bits(full.at[block], bits)
+        moves.append((pltpu.make_async_copy(source, here, sems.at[0, index]),
+                      remote(source, here, (sems.at[1, index], sems.at[2, index]), (1 - core, chip))))
+
+    def begin():
+        for local, far in moves:
+            local.start()
+            far.start()
+
+    def finish_sender():
+        for local, far in moves:
+            local.wait()
+            far.wait_send()
+
+    def finish_other():
+        for local, far in moves:
+            far.wait_recv()
+
+    return begin, finish_sender, finish_other
+
+
+def front_kernel(
+    x_ref, half_ref, down_ref, gain_ref, shift_ref, bias_ref, start_ref,
+    projected_ref, normed_ref, context_ref, lse_ref, wqkv_ref, wo_ref, wup_ref, wdown_ref,
+    seed_q, seed_o, seed_u, seed_d, chain_q, chain_o, chain_u, chain_d, pass_q, pass_o, pass_u, pass_d,
+):
+    core, chip, bits = place()
+    rows, width = x_ref.shape
+    cq, co, cu = width // 2, width // 6, 2 * width // 3
+    cq = 3 * width // 6
+    cd = width // 3
+    is_first = core == 0
+    q_begin, q_sent, q_got = seed(
+        [(half_ref.at[:, b * cq : (b + 1) * cq], b) for b in range(6)], wqkv_ref, None, seed_q, None)
+    o_begin, o_sent, o_got = seed(
+        [(half_ref.at[:, 3 * width + b * co : 3 * width + (b + 1) * co], b) for b in range(6)], wo_ref, None, seed_o, None)
+    u_begin, u_sent, u_got = seed(
+        [(half_ref.at[:, b * cu : (b + 1) * cu], b) for b in range(6)], wup_ref, None, seed_u, None)
+
+    def chains(full, sems, passes):
+        return [
+            Gather(full.at[3 * core + k], full.at[3 * (1 - core) + k], CHAINS[k], sems.at[k], passes.at[k])
+            for k in range(3)
+        ]
+
+    q_chains = chains(wqkv_ref, chain_q, pass_q)
+    o_chains = chains(wo_ref, chain_o, pass_o)
+    u_chains = chains(wup_ref, chain_u, pass_u)
+    d_chains = chains(wdown_ref, chain_d, pass_d)
+
+    greet()
+
+    @pl.when(is_first)
+    def _():
+        q_begin()
+
+    d_moves = []
+    for k in range(3):
+        source = down_ref.at[:, k * cd : (k + 1) * cd]
+        here = at_bits(wdown_ref.at[3 * core + k], bits)
+        d_moves.append((pltpu.make_async_copy(source, here, seed_d.at[0, k]),
+                        remote(source, here, (seed_d.at[1, k], seed_d.at[2, k]), (1 - core, chip))))
+    for local, far in d_moves:
+        local.start()
+        far.start()
+
+    @pl.when(is_first)
+    def _():
+        o_begin()
+
+    @pl.when(core == 1)
+    def _():
+        u_begin()
+
+    @pl.when(is_first)
+    def _():
+        q_sent()
+
+    @pl.when(core == 1)
+    def _():
+        q_got()
+
+    for chain in q_chains:
+        chain.step(0).start()
+
+    hat, _ = normalized(x_ref[...].astype(F32))
+    normed_ref[...] = (hat * gain_ref[...] + shift_ref[...]).astype(BF16)
+
+    for stage in range(BITS - 1):
+        for chain in q_chains:
+            chain.arrive(stage)
+
+    @pl.when(is_first)
+    def _():
+        o_sent()
+        u_got()
+
+    @pl.when(core == 1)
+    def _():
+        u_sent()
+        o_got()
+
+    for local, far in d_moves:
+        local.wait()
+        far.wait()
+    late = [chain for group in zip(u_chains, o_chains, d_chains) for chain in group]
+    for chain in late:
+        chain.step(0).start()
+
+    for chain in q_chains:
+        chain.arrive(BITS - 1)
+    for chain in late:
+        chain.arrive(0)
+    for stage in range(BITS):
+        for chain in q_chains:
+            chain.passed(stage)
+
+    normed = normed_ref[...]
+    for b in range(6):
+        cols = slice(b * cq, (b + 1) * cq)
+        weight = wqkv_ref[b].reshape(width, cq)
+        projected_ref[:, cols] = (nn(normed, weight) + bias_ref[:, cols]).astype(BF16)
+
+    pairs = width // PAIR
+    for chain in late:
+        chain.arrive(1)
+
+    def one_pair(pair, carry):
+        at_q = pl.ds(pl.multiple_of(pair * PAIR, PAIR), PAIR)
+        at_k = pl.ds(pl.multiple_of(width + pair * PAIR, PAIR), PAIR)
+        at_v = pl.ds(pl.multiple_of(2 * width + pair * PAIR, PAIR), PAIR)
+        query_t = (projected_ref[:, at_q].astype(F32) * HEAD_DIM**-0.5).T.astype(BF16)
+        key = projected_ref[:, at_k]
+        value_t = projected_ref[:, at_v].astype(F32).T.astype(BF16)
+        for block in range(rows // BLOCK):
+            at = slice(block * BLOCK, (block + 1) * BLOCK)
+            keys = (block + 1) * BLOCK
+            start = start_ref[:, at]
+            outs = []
+            for head in range(2):
+                scores = masked_scores(key, head_rows(query_t[:, at], head), start, block)
+                peak = jnp.max(scores, axis=0, keepdims=True)
+                raised = jnp.exp(scores - peak)
+                total = jnp.sum(raised, axis=0, keepdims=True)
+                lanes = slice(head * HEAD_DIM, (head + 1) * HEAD_DIM)
+                probs = (raised * (1.0 / total)).astype(BF16)
+                outs.append(nn(value_t[lanes, :keys], probs))
+                lse_ref[pair, head : head + 1, at] = peak + jnp.log(total)
+            context_ref[at, at_q] = jnp.concatenate(outs, axis=0).T
+
+        @pl.when(pair == 2)
+        def _():
+            for chain in late:
+                chain.arrive(2)
+
+        return carry
+
+    lax.fori_loop(0, pairs, one_pair, 0)
+
+    for chain in late:
+        chain.arrive(3)
+    for stage in range(BITS):
+        for chain in late:
+            chain.passed(stage)
+    for chain in q_chains + late:
+        chain.drain()
+
+
+def front(x, half, down, gain, shift, bias, start):
+    rows, width = x.shape
+    mine = half.shape[0]
+    mine_down = down.shape[0]
+    box = (2,) * BITS
+    pairs = width // PAIR
+    anywhere = pl.BlockSpec(memory_space=pl.ANY)
+    vmem = pl.BlockSpec(memory_space=pltpu.VMEM)
+    dma = pltpu.SemaphoreType.DMA
+    return pl.pallas_call(
+        front_kernel,
+        in_specs=[vmem, anywhere, anywhere, vmem, vmem, vmem, vmem],
+        out_specs=[vmem, vmem, vmem, vmem, vmem, anywhere, anywhere, anywhere],
+        out_shape=[
+            jax.ShapeDtypeStruct((rows, 3 * width), BF16),
+            jax.ShapeDtypeStruct((rows, width), BF16),
+            jax.ShapeDtypeStruct((rows, width), F32),
+            jax.ShapeDtypeStruct((pairs, 2, rows), F32),
+            jax.ShapeDtypeStruct((6,) + box + (mine, width // 2), BF16),
+            jax.ShapeDtypeStruct((6,) + box + (mine, width // 6), BF16),
+            jax.ShapeDtypeStruct((6,) + box + (mine, 2 * width // 3), BF16),
+            jax.ShapeDtypeStruct((6,) + box + (mine_down, width // 3), BF16),
+        ],
+        scratch_shapes=[dma((3, 6))] * 3 + [dma((3, 3))] + [dma((3, 2, BITS))] * 8,
+        compiler_params=params(collective_id=1, has_side_effects=True),
+        name="front",
+    )(x, half, down, gain, shift, bias, start)
+
+
+def one_batch(x, dy, lengths_row, attend_all, vectors):
     (pre_gain, pre_shift, query_bias, value_bias, sub_gain, sub_shift, out_bias,
      ffn_gain, ffn_shift, up_bias, mid_gain, mid_shift, down_bias) = [v[None, :] for v in vectors]
     count, width = x.shape
     alive, start = row_marks(lengths_row, count)
     bias = jnp.concatenate([query_bias, jnp.zeros_like(query_bias), value_bias], axis=1)
-    projected, normed = project(x, attention_block, pre_gain, pre_shift, bias)
-    context, lse = attend(projected, start)
+    projected, normed, context, lse, qkv, out_weight, up_weight, down_weight = attend_all(
+        x, pre_gain, pre_shift, bias, start
+    )
     out, ghid, gctx, mixed, gbranch, nffn, gup, mid, gffn, narrow, wide = middle(
-        x, dy, context, alive, attention_block, up_weight, down_weight,
+        x, dy, context, alive, out_weight, up_weight, down_weight,
         (sub_gain, sub_shift, out_bias, ffn_gain, ffn_shift, up_bias, mid_gain, mid_shift, down_bias),
     )
     grad_up = outer(nffn, gup, 256, F32, "outer_up")
     grad_down = outer(mid, gffn, 512, F32, "outer_down")
     dq, dk, dv = attend_back(projected, gctx, context, lse, start)
     grad_out = outer(mixed, gbranch, 256, F32, "outer_out")
-    grad_x, pre = project_back(dq, dk, dv, attention_block, x, ghid, pre_gain)
+    grad_x, pre = project_back(dq, dk, dv, qkv, x, ghid, pre_gain)
     grads = [outer(normed, d, 256, F32, "outer_qkv") for d in (dq, dk, dv)]
     grad_attention = jnp.concatenate(grads + [grad_out], axis=1)
     small = (pre[0], pre[1], pre[2], pre[3], narrow[0], narrow[1], narrow[2], narrow[3], narrow[4],
@@ -412,9 +696,40 @@
     hidden_units = half_weights.shape[2]
     shares = sections * lax.axis_size("dp")
 
-    blocks = lax.all_gather(half_weights[0], both, axis=0, tiled=True)
-    blocks = blocks.reshape(sections, width, hidden_units)
-    down_full = lax.all_gather(down_weight, both, axis=0, tiled=True)
+    fused = (
+        sections == 2
+        and shares == sections << BITS
+        and own_batches == 1
+        and half_weights.shape[1] % 16 == 0
+        and down_weight.shape[0] % 16 == 0
+    )
+    if fused:
+
+        def attend_all(x, gain, shift, bias, start):
+            *rest, qkv, out_weight, up_weight, down_full = front(
+                x, half_weights[0], down_weight, gain, shift, bias, start
+            )
+            blocks = [w.reshape(6, -1, w.shape[-1]) for w in (qkv, out_weight, up_weight, down_full)]
+            return (*rest, *blocks)
+
+    else:
+        blocks = lax.all_gather(half_weights[0], both, axis=0, tiled=True)
+        blocks = blocks.reshape(sections, width, hidden_units)
+        down_full = lax.all_gather(down_weight, both, axis=0, tiled=True)
+
+        def in_blocks(array):
+            return array.reshape(array.shape[0], 6, -1).transpose(1, 0, 2)
+
+        out_weight = in_blocks(blocks[0][:, 3 * width :])
+        up_weight = in_blocks(blocks[1])
+        down_blocks = down_full.reshape(2, -1, 3, width // 3).transpose(0, 2, 1, 3)
+        down_blocks = down_blocks.reshape(6, -1, width // 3)
+        qkv = blocks[0][:, : 3 * width]
+
+        def attend_all(x, gain, shift, bias, start):
+            projected, normed = project(x, qkv, gain, shift, bias)
+            context, lse = attend(projected, start)
+            return projected, normed, context, lse, in_blocks(qkv), out_weight, up_weight, down_blocks
 
     def own(array, rows):
         return lax.dynamic_slice_in_dim(array, section * rows, rows, axis=0)
@@ -425,7 +740,7 @@
     rows, sums = [], None
     for index in range(own_batches):
         at = slice(index * count, (index + 1) * count)
-        row, more = one_batch(x_rows[at], dy_rows[at], lengths[index], blocks[0], blocks[1], down_full, all_vectors)
+        row, more = one_batch(x_rows[at], dy_rows[at], lengths[index], attend_all, all_vectors)
         rows.append(row)
         sums = more if sums is None else jax.tree.map(jnp.add, sums, more)
     out_block = jnp.concatenate([row[0] for row in rows], axis=0)

time: 756 us -> 702 us (0.929)
  waiting for transfers between devices: 511 us -> 413 us
  Pallas kernels: 163 us -> 214 us
    all_gather x2 -> x0, waiting for transfers between devices: 84.6 us -> none  [the longest x1 67.5 us: shards(): blocks = lax.all_gather(half_weights[0], both, axis=0, tiled=True)]
    pallas_call x2 -> x1, Pallas kernels: 39.7 us -> 91.3 us  [front(): pl.pallas_call(front_kernel, in_specs=[vmem, anywhere, anywhere, vmem, vm...]
    all_gather x1, waiting for transfers between devices: 17.1 us -> 0.02 us  [shards(): layer_out = lax.all_gather(out_block, 'section', axis=0, tiled=True)]
    slice x1 -> x0, local copies, waits for them, and re-layouts: 8.28 us -> none  [shards(): blocks[1]]
    unnamed x7 -> x5, waiting for transfers between devices: 54.1 us -> 56.3 us
  transfers between devices with their start and end apart: 6 -> 5, of which waited for: 6 -> 4; matrix products, arithmetic and copies ran while one was open for 6% -> 3% of each run, Pallas kernels for 11% -> 6%
where the time goes in v3:
time: 702 us; the launch traced here: 701 us
  waiting for transfers between devices  413 us (59%)
  Pallas kernels  214 us (30%)
  local copies, waits for them, and re-layouts  34.1 us (5%)
  other arithmetic  20 us (3%)
  between operations  15.4 us (2%)
    reduce_scatter x1, waiting for transfers between devices, shards(): lax.psum_scatter(jnp.concatenate([grad_attention, grad_up], axis=0), both...  212 us
    reduce_scatter x1, waiting for transfers between devices, shards(): lax.psum_scatter(grad_down, both, scatter_dimension=0, tiled=True)  141 us
    pallas_call x1, Pallas kernels, front(): pl.pallas_call(front_kernel, in_specs=[vmem, anywhere, anywhere, vmem, vm...  91.3 us
    unnamed x5, waiting for transfers between devices  56.3 us
    pallas_call x1, Pallas kernels, middle(): pl.pallas_call(middle_kernel, grid=(rows // BLOCK,), in_specs=[row, row,...  45 us
    pallas_call x6, Pallas kernels, outer(): pl.pallas_call(outer_kernel, grid=(across // tile,), in_specs=[pl.BlockSp...  42 us
    pallas_call x1, Pallas kernels, attend_back(): pl.pallas_call(attend_back_kernel, grid=(pairs,), in_specs=[pair, pl.Bloc...  25.6 us
    concatenate x1, other arithmetic, shards(): jnp.concatenate([grad_attention, grad_up], axis=0)  15.8 us
  transfers between devices with their start and end apart: 5, of which 4 were waited for; matrix products, arithmetic and copies ran while one was open for 3% of the time, Pallas kernels for 6%

profile of v3, /device:TPU:0, one launch (start us, length us, event | category | flops | bytes accessed | tf_op | source)
XLA Modules:
  0.0 700.7 jit_solution(17985717733103162878)
XLA Ops:
  9.5 1.5 fusion.alive_ref
  23.9 3.7 constant_dynamic-slice_fusion.1
  28.2 91.3 %front.1 = (bf16[1024,2304]{1,0:T(8,128)(2,1)}, bf16[1024,768]{1,0:T(8,128)(2,1)}, f32[1024,768]{1,0:T(8,128)}, f32[6,2,1024]{2,1,0:T(2,128)}, bf16[6,2,2,2,2,48...) custom-call(bf16[1024,768]{1,0:T(8,128)(2,1)} %get-tuple-element.92., ...), custom_call_target="tpu_custom_call" | custom-call | tf_op jit(solution)/shard_map/front/pallas_call | solution.py:642
  119.5 45.0 %middle.1 = (f32[1024,768]{1,0:T(8,128)}, bf16[1024,768]{1,0:T(8,128)(2,1)}, bf16[1024,768]{1,0:T(8,128)(2,1)}, bf16[1024,768]{1,0:T(8,128)(2,1)}, bf16[1024,768...) custom-call(bf16[1024,768]{1,0:T(8,128)(2,1)} %get-tuple-element.92., ...), custom_call_target="tpu_custom_call" | custom-call | tf_op jit(solution)/shard_map/middle/pallas_call | solution.py:308
  164.5 25.6 %attend_back.1 = (bf16[1024,768]{1,0:T(8,128)(2,1)}, bf16[1024,768]{1,0:T(8,128)(2,1)}, bf16[1024,768]{1,0:T(8,128)(2,1)}) custom-call(bf16[1024,2304]{1,0:T(8,128)(2,1)} %get-tuple-element.46.q_ref.k_ref.v_ref, bf16[1024,2304]{1,0:T(8,128)(2,1)} %get-tuple-element.46.q_ref.k_ref.v_ref, bf16[1024,2304]{1,0:T(8,128)(2,1)} %get-tuple-element.46.q_ref.k_ref.v_ref, ...), custom_call_target="tpu_custom_call" | custom-call | tf_op jit(solution)/shard_map/attend_back/pallas_call | solution.py:214
  190.1 9.9 %project_back.1 = (f32[1024,768]{1,0:T(8,128)}, f32[8,768]{1,0:T(8,128)}) custom-call(bf16[1024,768]{1,0:T(8,128)(2,1)} %get-tuple-element.49.dq_ref.right_ref, bf16[1024,768]{1,0:T(8,128)(2,1)} %get-tuple-element.50.dk_ref.right_ref, bf16[1024,768]{1,0:T(8,128)(2,1)} %get-tuple-element.51.dv_ref.right_ref, bf16[6,768,384]{2,1,0:T(8,128)(2,1)} %bitcast.49, ...), custom_call_target="tpu_custom_call" | custom-call | tf_op jit(solution)/shard_map/project_back/pallas_call | solution.py:371
  204.6 10.8 %outer_down.1 = f32[3072,768]{1,0:T(8,128)} custom-call(bf16[1024,3072]{1,0:T(8,128)(2,1)} %get-tuple-element.60.left_ref, bf16[1024,768]{1,0:T(8,128)(2,1)} %get-tuple-element.61.right_ref), custom_call_target="tpu_custom_call" | custom-call | tf_op jit(solution)/shard_map/outer_down/pallas_call | solution.py:337
  215.5 5.5 outer_qkv.3
  221.0 5.2 outer_qkv.4
  226.2 5.1 outer_qkv.5
  231.2 5.1 outer_out.1
  236.3 10.4 %outer_up.1 = f32[768,3072]{1,0:T(8,128)} custom-call(bf16[1024,768]{1,0:T(8,128)(2,1)} %get-tuple-element.58.left_ref, bf16[1024,3072]{1,0:T(8,128)(2,1)} %get-tuple-element.59.right_ref), custom_call_target="tpu_custom_call" | custom-call | tf_op jit(solution)/shard_map/outer_up/pallas_call | solution.py:337
  246.7 15.8 %pad_maximum_fusion = f32[1536,3072]{1,0:T(8,128)} fusion(f32[768,3072]{1,0:T(8,128)} %outer_up.1, f32[768,768]{1,0:T(8,128)} %outer_out.1, f32[768,768]{1,0:T(8,128)} %outer_qkv.5, f32[768,768]{1,0:T(8,128)} %outer_qkv.4, f32[768,768]{1,0:T(8,128)S(1)} %copy-done.2), kind=kLoop, calls=%fused_computation | loop fusion | flops 18874368 | bytes 37748736 | tf_op jit(solution)/shard_map/concatenate | solution.py:751
  262.5 1.9 copy-done.3
  264.4 1.9 copy.41
  266.3 4.0 all-to-all-start
  270.2 3.7 all-to-all-done
  274.0 55.8 %all-reduce.3.cloned.1.call-done = f32[32,528]{1,0:T(8,128)} async-done(((f32[32,528]{1,0:T(8,128)}), f32[32,528]{1,0:T(8,128)}) %all-reduce.3.cloned.1.call-update) | async-done | bytes 67600
  329.7 1.4 dynamic-slice_bitcast_fusion.1
  331.1 1.6 dynamic-slice_bitcast_fusion
  332.7 141.1 %reduce-scatter.5.cloned.1.call-done = f32[96,768]{1,0:T(8,128)} async-done(((f32[3072,768]{1,0:T(8,128)}), f32[96,768]{1,0:T(8,128)}) %reduce-scatter.5.cloned.1.call-update) | async-done | bytes 294928 | tf_op jit(solution)/shard_map/reduce_scatter | solution.py:753
  473.9 212.2 %reduce-scatter.3.cloned.1.call-done = f32[48,3072]{1,0:T(8,128)} async-done(((f32[1536,3072]{1,0:T(8,128)}), f32[48,3072]{1,0:T(8,128)}) %reduce-scatter.3.cloned.1.call-update) | async-done | bytes 589840 | tf_op jit(solution)/shard_map/reduce_scatter | solution.py:750
  686.0 5.9 copy.45
  691.9 1.7 copy.46
  (53 shorter events, 19.5 us)
Async XLA Ops:
  8.0 0.7 copy-start
  8.0 321.7 %all-reduce.3.cloned.1.call-start = ((), (), s32[]{:S(2)}) async-start(), calls=%async_computation.6 | async-start | bytes 163840
  190.1 12.5 %copy-start.4 = (f32[8,768]{1,0:T(8,128)S(1)}, f32[8,768]{1,0:T(8,128)}, u32[]{:S(2)}) copy-start(f32[8,768]{1,0:T(8,128)} %get-tuple-element.63) | copy-start | bytes 73732
  204.0 128.7 %all-gather.2.cloned.1.call-start = ((), (), s32[]{:S(2)}) async-start(), calls=%async_computation.3 | async-start | bytes 9437184 | tf_op jit(solution)/shard_map/all_gather | solution.py:762
  204.6 269.3 %reduce-scatter.5.cloned.1.call-start = ((), (), s32[]{:S(2)}) async-start(), calls=%async_computation.5 | async-start | bytes 9732096 | tf_op jit(solution)/shard_map/reduce_scatter | solution.py:753
  215.4 470.6 %reduce-scatter.3.cloned.1.call-start = ((), (), s32[]{:S(2)}) async-start(), calls=%async_computation.4 | async-start | bytes 19464192 | tf_op jit(solution)/shard_map/reduce_scatter | solution.py:750
  236.3 10.4 %copy-start.2 = (f32[768,768]{1,0:T(8,128)S(1)}, f32[768,768]{1,0:T(8,128)}, u32[]{:S(2)}) copy-start(f32[768,768]{1,0:T(8,128)} %outer_qkv.3) | copy-start | bytes 7077892
  262.5 1.9 copy-start.3
  266.3 7.7 %all-to-all-start = ((f32[1024,2,384]{2,0,1:T(8,128)}), f32[1024,2,384]{2,0,1:T(8,128)S(1)}, u32[]{:S(2)}, u32[]{:S(2)}) async-start(f32[1024,2,384]{2,0,1:T(8,128)} %bitcast.46), calls=%async_computation | async-start | bytes 6291456 | tf_op jit(solution)/shard_map/all_to_all | solution.py:763
  686.0 7.6 %copy-start.1 = (s32[2,8]{1,0:T(2,128)S(1)}, s32[2,8]{1,0:T(2,128)}, u32[]{:S(2)}) copy-start(s32[2,8]{1,0:T(2,128)} %param.20) | copy-start | bytes 196
Sparse Core Ops, SparseCore 0:
  204.1 125.5 all-reduce.2
  336.2 137.5 reduce-scatter.4
  482.0 204.0 reduce-scatter.2
Sparse Core Ops, SparseCore 1:
  206.6 20.0 all-gather.1

commit v4 on v3

--- a/solution.py
+++ b/solution.py
@@ -52,12 +52,20 @@
     return pltpu.CompilerParams(vmem_limit_bytes=VMEM_LIMIT, **more)
 
 
-def side_by_side(ref):
-    return jnp.concatenate([ref[b] for b in range(6)], axis=1)
-
-
-def stacked(ref):
-    return jnp.concatenate([jnp.concatenate([ref[3 * h + k] for k in range(3)], axis=1) for h in range(2)], axis=0)
+def split_rest(ref):
+    _, width, columns = ref.shape
+    cu, co, cd = 4 * columns // 9, columns // 9, 2 * columns // 9
+    up = jnp.concatenate([ref[b, :, :cu] for b in range(6)], axis=1)
+    out = jnp.concatenate([ref[b, :, cu : cu + co] for b in range(6)], axis=1)
+    halves = []
+    for h in range(2):
+        parts = []
+        for n in range(2):
+            at = cu + co + n * cd
+            part = jnp.concatenate([ref[3 * h + k, :, at : at + cd] for k in range(3)], axis=1)
+            parts.append(part.reshape(1 << BITS, 1, width >> BITS, width))
+        halves.append(jnp.concatenate(parts, axis=1).reshape(2 * width, width))
+    return out, up, jnp.concatenate(halves, axis=0)
 
 
 def whole(shape):
@@ -123,12 +131,10 @@
     return jnp.where(ok, scores, -1e30)
 
 
-def attend_kernel(q_ref, k_ref, v_ref, start_ref, out_ref, lse_ref):
-    rows = q_ref.shape[0]
-    query_t = (q_ref[...].astype(F32) * HEAD_DIM**-0.5).T.astype(BF16)
-    key = k_ref[...]
-    value_t = v_ref[...].astype(F32).T.astype(BF16)
-    for block in range(rows // BLOCK):
+def attend_pair(query, key, value, start_ref, out_ref, lse_ref):
+    query_t = (query.astype(F32) * HEAD_DIM**-0.5).T.astype(BF16)
+    value_t = value.astype(F32).T.astype(BF16)
+    for block in range(query.shape[0] // BLOCK):
         at = slice(block * BLOCK, (block + 1) * BLOCK)
         keys = (block + 1) * BLOCK
         start = start_ref[:, at]
@@ -141,8 +147,12 @@
             lanes = slice(head * HEAD_DIM, (head + 1) * HEAD_DIM)
             probs = (raised * (1.0 / total)).astype(BF16)
             outs.append(nn(value_t[lanes, :keys], probs))
-            lse_ref[0, head : head + 1, at] = peak + jnp.log(total)
+            lse_ref[head : head + 1, at] = peak + jnp.log(total)
         out_ref[at, :] = jnp.concatenate(outs, axis=0).T
+
+
+def attend_kernel(q_ref, k_ref, v_ref, start_ref, out_ref, lse_ref):
+    attend_pair(q_ref[...], k_ref[...], v_ref[...], start_ref, out_ref, lse_ref.at[0])
 
 
 def attend(projected, start):
@@ -171,22 +181,18 @@
     )(projected, projected, projected, start)
 
 
-def attend_back_kernel(q_ref, k_ref, v_ref, g_ref, o_ref, lse_ref, start_ref, dq_ref, dk_ref, dv_ref, dk_acc, dv_acc):
-    rows = q_ref.shape[0]
+def attend_back_pair(query, key, value, grad, context, lse_ref, start_ref, dq_ref, dk_ref, dv_ref, dk_acc, dv_acc):
     scale = HEAD_DIM**-0.5
-    scaled = q_ref[...].astype(F32) * scale
+    scaled = query.astype(F32) * scale
     query = scaled.astype(BF16)
     query_t = scaled.T.astype(BF16)
-    key = k_ref[...]
     key_t = key.astype(F32).T.astype(BF16)
-    value = v_ref[...]
-    grad = g_ref[...]
     grad_f = grad.astype(F32)
     grad_t = grad_f.T.astype(BF16)
-    weighted_t = (grad_f * o_ref[...]).T
+    weighted_t = (grad_f * context).T
     dk_acc[...] = jnp.zeros_like(dk_acc)
     dv_acc[...] = jnp.zeros_like(dv_acc)
-    for block in range(rows // BLOCK):
+    for block in range(query.shape[0] // BLOCK):
         at = slice(block * BLOCK, (block + 1) * BLOCK)
         keys = (block + 1) * BLOCK
         start = start_ref[:, at]
@@ -195,7 +201,7 @@
             lanes = slice(head * HEAD_DIM, (head + 1) * HEAD_DIM)
             inner = col_sum(weighted_t[lanes, at])
             scores = masked_scores(key, head_rows(query_t[:, at], head), start, block)
-            soft = jnp.exp(scores - lse_ref[0, head : head + 1, at])
+            soft = jnp.exp(scores - lse_ref[head : head + 1, at])
             grad_soft = nn(value[:keys], head_rows(grad_t[:, at], head))
             grad_scores = (soft * (grad_soft - inner)).astype(BF16)
             dv_acc[:keys, :] += nn(soft.astype(BF16), head_cols(grad[at], head))
@@ -204,6 +210,13 @@
         dq_ref[at, :] = (jnp.concatenate(outs, axis=0) * scale).T.astype(BF16)
     dk_ref[...] = dk_acc[...].astype(BF16)
     dv_ref[...] = dv_acc[...].astype(BF16)
+
+
+def attend_back_kernel(q_ref, k_ref, v_ref, g_ref, o_ref, lse_ref, start_ref, dq_ref, dk_ref, dv_ref, dk_acc, dv_acc):
+    attend_back_pair(
+        q_ref[...], k_ref[...], v_ref[...], g_ref[...], o_ref[...], lse_ref.at[0], start_ref,
+        dq_ref, dk_ref, dv_ref, dk_acc, dv_acc,
+    )
 
 
 def attend_back(projected, grad_context, context, lse, start):
@@ -238,7 +251,7 @@
 
 
 def middle_kernel(
-    x_ref, dy_ref, ctx_ref, alive_ref, wo_ref, wu_ref, wd_ref,
+    x_ref, dy_ref, ctx_ref, alive_ref, rest_ref,
     sg_ref, ss_ref, ob_ref, fg_ref, fs_ref, ub_ref, mg_ref, ms_ref, db_ref,
     out_ref, ghid_ref, gctx_ref, mixed_ref, gbranch_ref, nffn_ref, gup_ref, mid_ref, gffn_ref,
     narrow_ref, wide_ref,
@@ -250,9 +263,7 @@
         narrow_ref[...] = jnp.zeros_like(narrow_ref)
         wide_ref[...] = jnp.zeros_like(wide_ref)
 
-    out_weight = side_by_side(wo_ref)
-    up_weight = side_by_side(wu_ref)
-    down_weight = stacked(wd_ref)
+    out_weight, up_weight, down_weight = split_rest(rest_ref)
     alive = alive_ref[...]
     ctx_hat, ctx_scale = normalized(ctx_ref[...])
     mixed = (ctx_hat * sg_ref[...] + ss_ref[...]).astype(BF16)
@@ -295,9 +306,9 @@
     narrow_ref[5:6, :] += col_sum(gffn.astype(F32))
 
 
-def middle(x, dy, context, alive, out_weight, up_weight, down_weight, vectors):
+def middle(x, dy, context, alive, rest, vectors):
     rows, width = x.shape
-    hidden = 6 * up_weight.shape[2]
+    hidden = 4 * width
     row = pl.BlockSpec((BLOCK, width), lambda i: (i, 0))
     row_wide = pl.BlockSpec((BLOCK, hidden), lambda i: (i, 0))
     once = dict(pipeline_mode=pl.Buffered(1))
@@ -311,9 +322,7 @@
         in_specs=[
             row, row, row,
             pl.BlockSpec((BLOCK, 1), lambda i: (i, 0)),
-            pl.BlockSpec(out_weight.shape, lambda i: (0, 0, 0), **once),
-            pl.BlockSpec(up_weight.shape, lambda i: (0, 0, 0), **once),
-            pl.BlockSpec(down_weight.shape, lambda i: (0, 0, 0), **once),
+            pl.BlockSpec(rest.shape, lambda i: (0, 0, 0), **once),
             narrow, narrow, narrow, narrow, narrow, wide, wide, wide, narrow,
         ],
         out_specs=[row, row, row, row, row, row, row_wide, row_wide, row, whole((8, width)), whole((8, hidden))],
@@ -324,7 +333,7 @@
         ],
         compiler_params=params(),
         name="middle",
-    )(x, dy, context, alive, out_weight, up_weight, down_weight, *vectors)
+    )(x, dy, context, alive, rest, *vectors)
 
 
 def outer_kernel(left_ref, right_ref, out_ref):
@@ -354,9 +363,7 @@
         narrow_ref[...] = jnp.zeros_like(narrow_ref)
 
     dq, dk, dv = dq_ref[...], dk_ref[...], dv_ref[...]
-    gnormed = sum(
-        nt(d, jnp.concatenate([w_ref[2 * n], w_ref[2 * n + 1]], axis=1)) for n, d in enumerate((dq, dk, dv))
-    )
+    gnormed = nt(dq, w_ref[:, :width]) + nt(dk, w_ref[:, width : 2 * width]) + nt(dv, w_ref[:, 2 * width :])
     hat, scale = normalized(x_ref[...].astype(F32))
     out_ref[...] = ghid_ref[...].astype(F32) + norm_back(hat, scale, gain_ref[...], gnormed)
     narrow_ref[0:1, :] += col_sum(gnormed * hat)
@@ -458,48 +465,60 @@
     pl.semaphore_wait(barrier, len(others))
 
 
-def seed(parts, full, me, sems, sender):
+def seed(parts, sems):
     core, chip, bits = place()
     moves = []
     for index, (source, block) in enumerate(parts):
-        here = at_bits(full.at[block], bits)
-        moves.append((pltpu.make_async_copy(source, here, sems.at[0, index]),
-                      remote(source, here, (sems.at[1, index], sems.at[2, index]), (1 - core, chip))))
+        here = at_bits(block, bits)
+        local = pltpu.make_async_copy(source, here, sems.at[0, index])
+        far = remote(source, here, (sems.at[1, index], sems.at[2, index]), (1 - core, chip))
+        moves.append((local, far))
 
     def begin():
         for local, far in moves:
             local.start()
             far.start()
 
-    def finish_sender():
+    def sent():
         for local, far in moves:
             local.wait()
             far.wait_send()
 
-    def finish_other():
-        for local, far in moves:
+    def got():
+        for _, far in moves:
             far.wait_recv()
 
-    return begin, finish_sender, finish_other
+    return begin, sent, got
 
 
 def front_kernel(
     x_ref, half_ref, down_ref, gain_ref, shift_ref, bias_ref, start_ref,
-    projected_ref, normed_ref, context_ref, lse_ref, wqkv_ref, wo_ref, wup_ref, wdown_ref,
-    seed_q, seed_o, seed_u, seed_d, chain_q, chain_o, chain_u, chain_d, pass_q, pass_o, pass_u, pass_d,
+    projected_ref, normed_ref, context_ref, lse_ref, wqkv_ref, rest_ref,
+    seed_q, seed_o, seed_u, seed_d, chain_q, chain_r, pass_q, pass_r,
 ):
     core, chip, bits = place()
     rows, width = x_ref.shape
-    cq, co, cu = width // 2, width // 6, 2 * width // 3
-    cq = 3 * width // 6
-    cd = width // 3
-    is_first = core == 0
+    mine = half_ref.shape[0]
+    cq, co, cu, cd = width // 2, width // 6, 2 * width // 3, width // 3
+    first = core == 0
+    second = core == 1
+    box = (slice(None),) * BITS
     q_begin, q_sent, q_got = seed(
-        [(half_ref.at[:, b * cq : (b + 1) * cq], b) for b in range(6)], wqkv_ref, None, seed_q, None)
+        [(half_ref.at[:, b * cq : (b + 1) * cq], wqkv_ref.at[b]) for b in range(6)], seed_q)
     o_begin, o_sent, o_got = seed(
-        [(half_ref.at[:, 3 * width + b * co : 3 * width + (b + 1) * co], b) for b in range(6)], wo_ref, None, seed_o, None)
+        [(half_ref.at[:, 3 * width + b * co : 3 * width + (b + 1) * co],
+          rest_ref.at[(b, *box, slice(None), slice(cu, cu + co))]) for b in range(6)], seed_o)
     u_begin, u_sent, u_got = seed(
-        [(half_ref.at[:, b * cu : (b + 1) * cu], b) for b in range(6)], wup_ref, None, seed_u, None)
+        [(half_ref.at[:, b * cu : (b + 1) * cu],
+          rest_ref.at[(b, *box, slice(None), slice(0, cu))]) for b in range(6)], seed_u)
+    d_begin, d_sent, d_got = seed(
+        [(down_ref.at[n * mine : (n + 1) * mine, k * cd : (k + 1) * cd],
+          rest_ref.at[(3 * core + k, *box, slice(None), slice(cu + co + n * cd, cu + co + (n + 1) * cd))])
+         for k in range(3) for n in range(2)], seed_d)
+    _, _, d_other = seed(
+        [(down_ref.at[n * mine : (n + 1) * mine, k * cd : (k + 1) * cd],
+          rest_ref.at[(3 * (1 - core) + k, *box, slice(None), slice(cu + co + n * cd, cu + co + (n + 1) * cd))])
+         for k in range(3) for n in range(2)], seed_d)
 
     def chains(full, sems, passes):
         return [
@@ -508,42 +527,15 @@
         ]
 
     q_chains = chains(wqkv_ref, chain_q, pass_q)
-    o_chains = chains(wo_ref, chain_o, pass_o)
-    u_chains = chains(wup_ref, chain_u, pass_u)
-    d_chains = chains(wdown_ref, chain_d, pass_d)
+    late = chains(rest_ref, chain_r, pass_r)
 
     greet()
-
-    @pl.when(is_first)
-    def _():
-        q_begin()
-
-    d_moves = []
-    for k in range(3):
-        source = down_ref.at[:, k * cd : (k + 1) * cd]
-        here = at_bits(wdown_ref.at[3 * core + k], bits)
-        d_moves.append((pltpu.make_async_copy(source, here, seed_d.at[0, k]),
-                        remote(source, here, (seed_d.at[1, k], seed_d.at[2, k]), (1 - core, chip))))
-    for local, far in d_moves:
-        local.start()
-        far.start()
-
-    @pl.when(is_first)
-    def _():
-        o_begin()
-
-    @pl.when(core == 1)
-    def _():
-        u_begin()
-
-    @pl.when(is_first)
-    def _():
-        q_sent()
-
-    @pl.when(core == 1)
-    def _():
-        q_got()
-
+    pl.when(first)(q_begin)
+    d_begin()
+    pl.when(first)(o_begin)
+    pl.when(second)(u_begin)
+    pl.when(first)(q_sent)
+    pl.when(second)(q_got)
     for chain in q_chains:
         chain.step(0).start()
 
@@ -554,23 +546,20 @@
         for chain in q_chains:
             chain.arrive(stage)
 
-    @pl.when(is_first)
+    @pl.when(first)
     def _():
         o_sent()
         u_got()
 
-    @pl.when(core == 1)
+    @pl.when(second)
     def _():
         u_sent()
         o_got()
 
-    for local, far in d_moves:
-        local.wait()
-        far.wait()
-    late = [chain for group in zip(u_chains, o_chains, d_chains) for chain in group]
+    d_sent()
+    d_other()
     for chain in late:
         chain.step(0).start()
-
     for chain in q_chains:
         chain.arrive(BITS - 1)
     for chain in late:
@@ -593,24 +582,10 @@
         at_q = pl.ds(pl.multiple_of(pair * PAIR, PAIR), PAIR)
         at_k = pl.ds(pl.multiple_of(width + pair * PAIR, PAIR), PAIR)
         at_v = pl.ds(pl.multiple_of(2 * width + pair * PAIR, PAIR), PAIR)
-        query_t = (projected_ref[:, at_q].astype(F32) * HEAD_DIM**-0.5).T.astype(BF16)
-        key = projected_ref[:, at_k]
-        value_t = projected_ref[:, at_v].astype(F32).T.astype(BF16)
-        for block in range(rows // BLOCK):
-            at = slice(block * BLOCK, (block + 1) * BLOCK)
-            keys = (block + 1) * BLOCK
-            start = start_ref[:, at]
-            outs = []
-            for head in range(2):
-                scores = masked_scores(key, head_rows(query_t[:, at], head), start, block)
-                peak = jnp.max(scores, axis=0, keepdims=True)
-                raised = jnp.exp(scores - peak)
-                total = jnp.sum(raised, axis=0, keepdims=True)
-                lanes = slice(head * HEAD_DIM, (head + 1) * HEAD_DIM)
-                probs = (raised * (1.0 / total)).astype(BF16)
-                outs.append(nn(value_t[lanes, :keys], probs))
-                lse_ref[pair, head : head + 1, at] = peak + jnp.log(total)
-            context_ref[at, at_q] = jnp.concatenate(outs, axis=0).T
+        attend_pair(
+            projected_ref[:, at_q], projected_ref[:, at_k], projected_ref[:, at_v], start_ref,
+            context_ref.at[:, at_q], lse_ref.at[pair],
+        )
 
         @pl.when(pair == 2)
         def _():
@@ -633,7 +608,6 @@
 def front(x, half, down, gain, shift, bias, start):
     rows, width = x.shape
     mine = half.shape[0]
-    mine_down = down.shape[0]
     box = (2,) * BITS
     pairs = width // PAIR
     anywhere = pl.BlockSpec(memory_space=pl.ANY)
@@ -642,34 +616,400 @@
     return pl.pallas_call(
         front_kernel,
         in_specs=[vmem, anywhere, anywhere, vmem, vmem, vmem, vmem],
-        out_specs=[vmem, vmem, vmem, vmem, vmem, anywhere, anywhere, anywhere],
+        out_specs=[vmem, vmem, vmem, vmem, vmem, anywhere],
         out_shape=[
             jax.ShapeDtypeStruct((rows, 3 * width), BF16),
             jax.ShapeDtypeStruct((rows, width), BF16),
             jax.ShapeDtypeStruct((rows, width), F32),
             jax.ShapeDtypeStruct((pairs, 2, rows), F32),
             jax.ShapeDtypeStruct((6,) + box + (mine, width // 2), BF16),
-            jax.ShapeDtypeStruct((6,) + box + (mine, width // 6), BF16),
-            jax.ShapeDtypeStruct((6,) + box + (mine, 2 * width // 3), BF16),
-            jax.ShapeDtypeStruct((6,) + box + (mine_down, width // 3), BF16),
-        ],
-        scratch_shapes=[dma((3, 6))] * 3 + [dma((3, 3))] + [dma((3, 2, BITS))] * 8,
+            jax.ShapeDtypeStruct((6,) + box + (mine, 3 * width // 2), BF16),
+        ],
+        scratch_shapes=[dma((3, 6))] * 4 + [dma((3, 2, BITS))] * 4,
         compiler_params=params(collective_id=1, has_side_effects=True),
         name="front",
     )(x, half, down, gain, shift, bias, start)
 
 
-def one_batch(x, dy, lengths_row, attend_all, vectors):
+ORDERS = tuple(tuple(reversed(chain)) for chain in CHAINS)
+
+
+def outer_rest_kernel(nffn_ref, gup_ref, mixed_ref, gbranch_ref, mid_ref, gffn_ref, out_ref, nffn_t, mixed_t, mid_t):
+    block = pl.program_id(0)
+    rows, width = nffn_ref.shape
+    cu, co, cd = 2 * width // 3, width // 6, width // 3
+
+    @pl.when(block == 0)
+    def _():
+        nffn_t[...] = nffn_ref[...].T
+        mixed_t[...] = mixed_ref[...].T
+
+    @pl.when(block % 3 == 0)
+    def _():
+        mid_t[...] = mid_ref[...].T
+
+    out_ref[0, :, :cu] = nn(nffn_t[...], gup_ref[...]).astype(BF16)
+    out_ref[0, :, cu : cu + co] = nn(mixed_t[...], gbranch_ref[...]).astype(BF16)
+    down = nn(mid_t[...], gffn_ref[...]).astype(BF16)
+    chips = 1 << BITS
+    down = down.reshape(chips, 2, width // chips, cd)
+    for n in range(2):
+        at = cu + co + n * cd
+        out_ref[0, :, at : at + cd] = down[:, n].reshape(width, cd)
+
+
+def outer_rest(nffn, gup, mixed, gbranch, mid, gffn):
+    rows, width = nffn.shape
+    cu, co, cd = 2 * width // 3, width // 6, width // 3
+    return pl.pallas_call(
+        outer_rest_kernel,
+        grid=(6,),
+        in_specs=[
+            whole((rows, width)),
+            pl.BlockSpec((rows, cu), lambda b: (0, b)),
+            whole((rows, width)),
+            pl.BlockSpec((rows, co), lambda b: (0, b)),
+            pl.BlockSpec((rows, 2 * width), lambda b: (0, b // 3)),
+            pl.BlockSpec((rows, cd), lambda b: (0, b % 3)),
+        ],
+        out_specs=pl.BlockSpec((1, width, 3 * width // 2), lambda b: (b, 0, 0)),
+        out_shape=jax.ShapeDtypeStruct((6, width, 3 * width // 2), BF16),
+        scratch_shapes=[
+            pltpu.VMEM((width, rows), BF16), pltpu.VMEM((width, rows), BF16), pltpu.VMEM((2 * width, rows), BF16)
+        ],
+        compiler_params=params(),
+        name="outer_rest",
+    )(nffn, gup, mixed, gbranch, mid, gffn)
+
+
+class Scatter:
+    def __init__(self, total, landings, order, sems, final):
+        self.total, self.landings, self.order, self.sems, self.final = total, landings, order, sems, final
+        self.core, self.chip, self.bits = place()
+
+    def send(self, stage):
+        values = [slice(None)] * BITS
+        for bit in self.order[:stage]:
+            values[bit] = self.bits[bit]
+        values[self.order[stage]] = 1 - self.bits[self.order[stage]]
+        device = (self.core, partner_of(self.chip, self.bits, self.order[stage]))
+        sems = (self.sems.at[0, stage], self.sems.at[1, stage])
+        return remote(at_bits(self.total, values), self.landings[stage], sems, device)
+
+    def arrive(self, stage):
+        self.send(stage).wait_recv()
+        landing = self.landings[stage]
+        values = [None] * BITS
+        for bit in self.order[: stage + 1]:
+            values[bit] = self.bits[bit]
+        free = [bit for bit in reversed(range(BITS)) if values[bit] is None]
+        if not free:
+            at = tuple(self.bits[bit] for bit in reversed(range(BITS)))
+            self.final[...] = self.total[at].astype(F32) + landing[...].astype(F32)
+            return
+        for index in range(1 << len(free)):
+            picks = [(index >> (len(free) - 1 - n)) & 1 for n in range(len(free))]
+            for bit, pick in zip(free, picks):
+                values[bit] = pick
+            at = tuple(values[bit] for bit in reversed(range(BITS)))
+            self.total[at] = self.total[at] + landing[tuple(picks)]
+        self.send(stage + 1).start()
+
+    def drain(self):
+        for stage in range(BITS):
+            self.send(stage).wait_send()
+
+
+def back_kernel(
+    projected_ref, gctx_ref, context_ref, lse_ref, start_ref, normed_ref, x_ref, ghid_ref, gain_ref, wqkv_ref,
+    narrow_ref, wide_ref, rest_ref, rows_ref,
+    layer_ref, grad_ref, half_ref, down_ref, slim_ref, broad_ref,
+    dproj, dk_acc, dv_acc, normed_t, far_rows,
+    total_r, first_r, r0, r1, r2, r3, final_r, other_r,
+    total_q, far_q, first_q, q0, q1, q2, q3, final_q, other_q,
+    small, small_in,
+    local_sems, swap_sems, chain_r, chain_q, small_sems,
+):
+    core, chip, bits = place()
+    rows, width = x_ref.shape
+    mine = half_ref.shape[0]
+    pairs = width // PAIR
+    cq, co, cu, cd = width // 2, width // 6, 2 * width // 3, width // 3
+    sibling = (1 - core, chip)
+    first = core == 0
+    second = core == 1
+
+    def swap(index, source, target):
+        return remote(source, target, (swap_sems.at[0, index], swap_sems.at[1, index]), sibling)
+
+    r_chains = [
+        Scatter(total_r.at[k], [r0.at[k], r1.at[k], r2.at[k], r3.at[k]], ORDERS[k], chain_r.at[k], final_r.at[k])
+        for k in range(3)
+    ]
+    q_chains = [
+        Scatter(total_q.at[k], [q0.at[k], q1.at[k], q2.at[k], q3.at[k]], ORDERS[k], chain_q.at[k], final_q.at[k])
+        for k in range(3)
+    ]
+
+    greet()
+    own_rest = pltpu.make_async_copy(rest_ref.at[pl.ds(3 * core, 3)], total_r, local_sems.at[0])
+    far_rest = swap(0, rest_ref.at[pl.ds(3 * (1 - core), 3)], first_r)
+    own_rows = pltpu.make_async_copy(rows_ref, layer_ref.at[core], local_sems.at[1])
+    out_rows = swap(1, rows_ref, layer_ref.at[core])
+    far_rest.start()
+    own_rest.start()
+    normed_t[...] = normed_ref[...].T
+
+    def begin(chains, total, landed):
+        for k, chain in enumerate(chains):
+            for index in range(1 << BITS):
+                at = (k,) + tuple((index >> bit) & 1 for bit in reversed(range(BITS)))
+                total[at] = total[at] + landed[at]
+            chain.send(0).start()
+
+    def one_pair(pair, carry):
+        @pl.when(pair == 1)
+        def _():
+            own_rest.wait()
+            far_rest.wait_recv()
+            begin(r_chains, total_r, first_r)
+            out_rows.start()
+            own_rows.start()
+
+        @pl.when(pair == 5)
+        def _():
+            for chain in r_chains:
+                chain.arrive(0)
+
+        at_q = pl.ds(pl.multiple_of(pair * PAIR, PAIR), PAIR)
+        at_k = pl.ds(pl.multiple_of(width + pair * PAIR, PAIR), PAIR)
+        at_v = pl.ds(pl.multiple_of(2 * width + pair * PAIR, PAIR), PAIR)
+        attend_back_pair(
+            projected_ref[:, at_q], projected_ref[:, at_k], projected_ref[:, at_v], gctx_ref[:, at_q],
+            context_ref[:, at_q], lse_ref.at[pair], start_ref,
+            dproj.at[:, at_q], dproj.at[:, at_k], dproj.at[:, at_v], dk_acc, dv_acc,
+        )
+        return carry
+
+    lax.fori_loop(0, pairs, one_pair, 0)
+
+    def qkv_block(block):
+        grad = dproj[:, pl.ds(pl.multiple_of(block * cq, PAIR), cq)]
+        return nn(normed_t[...], grad).astype(BF16).reshape((2,) * BITS + (mine, cq))
+
+    for k in range(3):
+        far_q[k] = qkv_block(3 * (1 - core) + k)
+    swap_q = swap(2, far_q, first_q)
+    swap_q.start()
+    for k in range(3):
+        total_q[k] = qkv_block(3 * core + k)
+    swap_q.wait_recv()
+    begin(q_chains, total_q, first_q)
+    for chain in r_chains:
+        chain.arrive(1)
+
+    small[0] = jnp.zeros_like(small[0])
+
+    def one_block(step, carry):
+        at = pl.ds(pl.multiple_of(step * BLOCK, BLOCK), BLOCK)
+        gnormed = jnp.zeros((BLOCK, width), F32)
+        for n in range(3):
+            weight = jnp.concatenate([wqkv_ref[2 * n + b].reshape(width, cq) for b in range(2)], axis=1)
+            gnormed = gnormed + nt(dproj[at, n * width : (n + 1) * width], weight)
+        hat, scale = normalized(x_ref[at, :].astype(F32))
+        grad_x = ghid_ref[at, :].astype(F32) + norm_back(hat, scale, gain_ref[...], gnormed)
+
+        @pl.when(first)
+        def _():
+            grad_ref[0, at, :] = grad_x[:, :cq]
+            far_rows[at, :] = grad_x[:, cq:]
+
+        @pl.when(second)
+        def _():
+            grad_ref[1, at, :] = grad_x[:, cq:]
+            far_rows[at, :] = grad_x[:, :cq]
+
+        small[0, 0:1, :] += col_sum(gnormed * hat)
+        small[0, 1:2, :] += col_sum(gnormed)
+        small[0, 2:3, :] += col_sum(dproj[at, :width].astype(F32))
+        small[0, 3:4, :] += col_sum(dproj[at, 2 * width :].astype(F32))
+        return carry
+
+    lax.fori_loop(0, rows // BLOCK, one_block, 0)
+    swap_x = swap(3, far_rows, grad_ref.at[core])
+    swap_x.start()
+    small[0, 4:10, :] = narrow_ref[0:6, :]
+    for n in range(3):
+        for part in range(4):
+            row = 10 + 4 * n + part
+            small[0, row : row + 1, :] = wide_ref[n : n + 1, part * width : (part + 1) * width]
+
+    def small_step(stage):
+        device = sibling if stage == 0 else (core, partner_of(chip, bits, stage - 1))
+        return remote(small.at[stage], small_in.at[stage], (small_sems.at[0, stage], small_sems.at[1, stage]), device)
+
+    def small_arrive(stage):
+        small_step(stage).wait_recv()
+        small[stage + 1] = small[stage] + small_in[stage]
+        if stage < BITS:
+            small_step(stage + 1).start()
+
+    small_step(0).start()
+    for chain in q_chains:
+        chain.arrive(0)
+    small_arrive(0)
+    for chain in r_chains:
+        chain.arrive(2)
+    for chain in q_chains:
+        chain.arrive(1)
+    small_arrive(1)
+    for chain in r_chains:
+        chain.arrive(3)
+    swap_r = swap(4, final_r, other_r)
+    swap_r.start()
+    for chain in q_chains:
+        chain.arrive(2)
+    small_arrive(2)
+    for k in range(3):
+        for n in range(2):
+            at = cu + co + n * cd
+            down_ref[n * mine : (n + 1) * mine, k * cd : (k + 1) * cd] = final_r[k, :, at : at + cd]
+    for chain in q_chains:
+        chain.arrive(3)
+    swap_f = swap(5, final_q, other_q)
+    swap_f.start()
+    small_arrive(3)
+    swap_r.wait_recv()
+    small_arrive(4)
+
+    sums = small[BITS + 1]
+    share = core * (1 << BITS) + chip
+
+    def pick(values, each):
+        lane = lax.broadcasted_iota(jnp.int32, (values.shape[1], 128), 0)
+        column = lax.broadcasted_iota(jnp.int32, (values.shape[1], 128), 1)
+        wanted = ((lane == share * each + column) & (column < each)).astype(F32)
+        return lax.dot_general(
+            values, wanted, (((1,), (0,)), ((), ())), precision=lax.Precision.HIGHEST, preferred_element_type=F32
+        )
+
+    shares = 2 << BITS
+    slim_ref[...] = pick(sums[0:16], width // shares)
+    broad_ref[...] = jnp.zeros_like(broad_ref)
+    for n in range(3):
+        row = jnp.concatenate([sums[10 + 4 * n + part : 11 + 4 * n + part] for part in range(4)], axis=1)
+        broad_ref[n : n + 1, :] = pick(jnp.broadcast_to(row, (8, 4 * width)), 4 * width // shares)[0:1]
+
+    swap_f.wait_recv()
+
+    @pl.when(first)
+    def _():
+        for k in range(3):
+            half_ref[:, k * cq : (k + 1) * cq] = final_q[k]
+            half_ref[:, (3 + k) * cq : (4 + k) * cq] = other_q[k]
+            half_ref[:, 3 * width + k * co : 3 * width + (k + 1) * co] = final_r[k, :, cu : cu + co]
+            half_ref[:, 3 * width + (3 + k) * co : 3 * width + (4 + k) * co] = other_r[k, :, cu : cu + co]
+
+    @pl.when(second)
+    def _():
+        for k in range(3):
+            half_ref[:, k * cu : (k + 1) * cu] = other_r[k, :, :cu]
+            half_ref[:, (3 + k) * cu : (4 + k) * cu] = final_r[k, :, :cu]
+
+    swap(3, far_rows, grad_ref.at[1 - core]).wait_recv()
+    swap(1, rows_ref, layer_ref.at[1 - core]).wait_recv()
+    own_rows.wait()
+    for done in (far_rest, out_rows, swap_q, swap_x, swap_r, swap_f):
+        done.wait_send()
+    for stage in range(BITS + 1):
+        small_step(stage).wait_send()
+    for chain in r_chains + q_chains:
+        chain.drain()
+
+
+def back(projected, gctx, context, lse, start, normed, x, ghid, gain, wqkv, narrow, wide, rest, out_rows):
+    rows, width = x.shape
+    box = (2,) * BITS
+    mine = width >> BITS
+    cq, cr = width // 2, 3 * width // 2
+    anywhere = pl.BlockSpec(memory_space=pl.ANY)
+    vmem = pl.BlockSpec(memory_space=pltpu.VMEM)
+    dma = pltpu.SemaphoreType.DMA
+
+    def held(*shape, dtype=BF16):
+        return pltpu.VMEM(shape, dtype)
+
+    def landings(columns):
+        return [held(3, *box[stage + 1 :], mine, columns) for stage in range(BITS)]
+
+    return pl.pallas_call(
+        back_kernel,
+        in_specs=[vmem] * 12 + [anywhere] * 2,
+        out_specs=[anywhere] + [vmem] * 5,
+        out_shape=[
+            jax.ShapeDtypeStruct((2, rows, width), F32),
+            jax.ShapeDtypeStruct((2, rows, cq), F32),
+            jax.ShapeDtypeStruct((mine, 4 * width), F32),
+            jax.ShapeDtypeStruct((2 * mine, width), F32),
+            jax.ShapeDtypeStruct((16, 128), F32),
+            jax.ShapeDtypeStruct((8, 128), F32),
+        ],
+        scratch_shapes=[
+            held(rows, 3 * width), held(rows, PAIR, dtype=F32), held(rows, PAIR, dtype=F32), held(width, rows),
+            held(rows, cq, dtype=F32),
+            held(3, *box, mine, cr), held(3, *box, mine, cr), *landings(cr),
+            held(3, mine, cr, dtype=F32), held(3, mine, cr, dtype=F32),
+            held(3, *box, mine, cq), held(3, *box, mine, cq), held(3, *box, mine, cq), *landings(cq),
+            held(3, mine, cq, dtype=F32), held(3, mine, cq, dtype=F32),
+            held(BITS + 2, 24, width, dtype=F32), held(BITS + 1, 24, width, dtype=F32),
+            dma((2,)), dma((2, 6)), dma((3, 2, BITS)), dma((3, 2, BITS)), dma((2, BITS + 1)),
+        ],
+        compiler_params=params(collective_id=2, has_side_effects=True),
+        name="back",
+    )(projected, gctx, context, lse, start, normed, x, ghid, gain, wqkv, narrow, wide,
+      rest.reshape((6,) + box + (mine, cr)), out_rows)
+
+
+def unpacked(vectors):
+    return [vector[None, :] for vector in vectors]
+
+
+def marks_and_bias(x, lengths_row, query_bias, value_bias):
+    alive, start = row_marks(lengths_row, x.shape[0])
+    bias = jnp.concatenate([query_bias, jnp.zeros_like(query_bias), value_bias], axis=1)
+    return alive, start, bias
+
+
+def fused_batch(x, dy, lengths_row, half, down, vectors):
     (pre_gain, pre_shift, query_bias, value_bias, sub_gain, sub_shift, out_bias,
-     ffn_gain, ffn_shift, up_bias, mid_gain, mid_shift, down_bias) = [v[None, :] for v in vectors]
+     ffn_gain, ffn_shift, up_bias, mid_gain, mid_shift, down_bias) = unpacked(vectors)
     count, width = x.shape
-    alive, start = row_marks(lengths_row, count)
-    bias = jnp.concatenate([query_bias, jnp.zeros_like(query_bias), value_bias], axis=1)
-    projected, normed, context, lse, qkv, out_weight, up_weight, down_weight = attend_all(
-        x, pre_gain, pre_shift, bias, start
+    alive, start, bias = marks_and_bias(x, lengths_row, query_bias, value_bias)
+    projected, normed, context, lse, wqkv, rest = front(x, half, down, pre_gain, pre_shift, bias, start)
+    out, ghid, gctx, mixed, gbranch, nffn, gup, mid, gffn, narrow, wide = middle(
+        x, dy, context, alive, rest.reshape(6, width, -1),
+        (sub_gain, sub_shift, out_bias, ffn_gain, ffn_shift, up_bias, mid_gain, mid_shift, down_bias),
     )
+    grads = outer_rest(nffn, gup, mixed, gbranch, mid, gffn)
+    layer, grad_x, half_grad, down_grad, slim, broad = back(
+        projected, gctx, context, lse, start, normed, x, ghid, pre_gain, wqkv, narrow, wide, grads, out
+    )
+    shares = 2 << BITS
+    slim = slim[:10, : width // shares]
+    broad = broad[:3, : 4 * width // shares]
+    small = (slim[0], slim[1], slim[2], slim[3], slim[4], slim[5], slim[6], slim[7], slim[8],
+             broad[0], broad[1], broad[2], slim[9])
+    return layer.reshape(-1, width), grad_x.reshape(-1, width // 2), half_grad[None], down_grad, *small
+
+
+def one_batch(x, dy, lengths_row, qkv, rest, vectors):
+    (pre_gain, pre_shift, query_bias, value_bias, sub_gain, sub_shift, out_bias,
+     ffn_gain, ffn_shift, up_bias, mid_gain, mid_shift, down_bias) = unpacked(vectors)
+    alive, start, bias = marks_and_bias(x, lengths_row, query_bias, value_bias)
+    projected, normed = project(x, qkv, pre_gain, pre_shift, bias)
+    context, lse = attend(projected, start)
     out, ghid, gctx, mixed, gbranch, nffn, gup, mid, gffn, narrow, wide = middle(
-        x, dy, context, alive, out_weight, up_weight, down_weight,
+        x, dy, context, alive, rest,
         (sub_gain, sub_shift, out_bias, ffn_gain, ffn_shift, up_bias, mid_gain, mid_shift, down_bias),
     )
     grad_up = outer(nffn, gup, 256, F32, "outer_up")
@@ -696,51 +1036,37 @@
     hidden_units = half_weights.shape[2]
     shares = sections * lax.axis_size("dp")
 
-    fused = (
+    def own(array, rows):
+        return lax.dynamic_slice_in_dim(array, section * rows, rows, axis=0)
+
+    x_rows = own(tokens, own_rows)
+    dy_rows = own(out_grad, own_rows)
+    lengths = own(seq_lengths, own_batches)
+    if (
         sections == 2
         and shares == sections << BITS
         and own_batches == 1
         and half_weights.shape[1] % 16 == 0
-        and down_weight.shape[0] % 16 == 0
-    )
-    if fused:
-
-        def attend_all(x, gain, shift, bias, start):
-            *rest, qkv, out_weight, up_weight, down_full = front(
-                x, half_weights[0], down_weight, gain, shift, bias, start
-            )
-            blocks = [w.reshape(6, -1, w.shape[-1]) for w in (qkv, out_weight, up_weight, down_full)]
-            return (*rest, *blocks)
-
-    else:
-        blocks = lax.all_gather(half_weights[0], both, axis=0, tiled=True)
-        blocks = blocks.reshape(sections, width, hidden_units)
-        down_full = lax.all_gather(down_weight, both, axis=0, tiled=True)
-
-        def in_blocks(array):
-            return array.reshape(array.shape[0], 6, -1).transpose(1, 0, 2)
-
-        out_weight = in_blocks(blocks[0][:, 3 * width :])
-        up_weight = in_blocks(blocks[1])
-        down_blocks = down_full.reshape(2, -1, 3, width // 3).transpose(0, 2, 1, 3)
-        down_blocks = down_blocks.reshape(6, -1, width // 3)
-        qkv = blocks[0][:, : 3 * width]
-
-        def attend_all(x, gain, shift, bias, start):
-            projected, normed = project(x, qkv, gain, shift, bias)
-            context, lse = attend(projected, start)
-            return projected, normed, context, lse, in_blocks(qkv), out_weight, up_weight, down_blocks
-
-    def own(array, rows):
-        return lax.dynamic_slice_in_dim(array, section * rows, rows, axis=0)
-
-    x_rows = own(tokens, own_rows)
-    dy_rows = own(out_grad, own_rows)
-    lengths = own(seq_lengths, own_batches)
+        and down_weight.shape[0] == 2 * half_weights.shape[1]
+        and hidden_units == 4 * width
+    ):
+        return fused_batch(x_rows, dy_rows, lengths[0], half_weights[0], down_weight, all_vectors)
+
+    blocks = lax.all_gather(half_weights[0], both, axis=0, tiled=True)
+    blocks = blocks.reshape(sections, width, hidden_units)
+    down_full = lax.all_gather(down_weight, both, axis=0, tiled=True)
+    qkv = blocks[0][:, : 3 * width]
+
+    def in_blocks(array):
+        return array.reshape(array.shape[0], 6, -1).transpose(1, 0, 2)
+
+    down_blocks = down_full.reshape(2, 1 << BITS, 2, width >> BITS, 3, width // 3).transpose(0, 4, 1, 3, 2, 5)
+    down_blocks = down_blocks.reshape(6, width, 2 * width // 3)
+    rest = jnp.concatenate([in_blocks(blocks[1]), in_blocks(blocks[0][:, 3 * width :]), down_blocks], axis=2)
     rows, sums = [], None
     for index in range(own_batches):
         at = slice(index * count, (index + 1) * count)
-        row, more = one_batch(x_rows[at], dy_rows[at], lengths[index], attend_all, all_vectors)
+        row, more = one_batch(x_rows[at], dy_rows[at], lengths[index], qkv, rest, all_vectors)
         rows.append(row)
         sums = more if sums is None else jax.tree.map(jnp.add, sums, more)
     out_block = jnp.concatenate([row[0] for row in rows], axis=0)

time: 702 us -> 314 us (0.45)
  waiting for transfers between devices: 413 us -> 0 us
  Pallas kernels: 214 us -> 279 us
  other arithmetic: 20 us -> 4.15 us
  between operations: 15.4 us -> 0.72 us
    reduce_scatter x2 -> x0, waiting for transfers between devices: 353 us -> none  [the longest x1 212 us: shards(): lax.psum_scatter(jnp.concatenate([grad_attention, grad_up], axis=0), both...]
    pallas_call x8 -> x2, Pallas kernels: 77.5 us -> 138 us  [the longest x1 116 us: back(): pl.pallas_call(back_kernel, in_specs=[vmem] * 12 + [anywhere] * 2, out_sp...]
    unnamed x5 -> x0, waiting for transfers between devices: 56.3 us -> none
    concatenate x2 -> x1, other arithmetic: 16.4 us -> 0.61 us  [marks_and_bias(): jnp.concatenate([query_bias, jnp.zeros_like(query_bias), value_bias], axi...]
  transfers between devices with their start and end apart: 5 -> 0, of which waited for: 4 -> 0; matrix products, arithmetic and copies ran while one was open for 3% -> 0% of each run, Pallas kernels for 6% -> 0%
where the time goes in v4:
time: 314 us; the launch traced here: 312 us
  Pallas kernels  279 us (89%)
  local copies, waits for them, and re-layouts  28.1 us (9%)
  other arithmetic  4.15 us (1%)
    pallas_call x1, Pallas kernels, back(): pl.pallas_call(back_kernel, in_specs=[vmem] * 12 + [anywhere] * 2, out_sp...  116 us
    pallas_call x1, Pallas kernels, front(): pl.pallas_call(front_kernel, in_specs=[vmem, anywhere, anywhere, vmem, vm...  96.7 us
    pallas_call x1, Pallas kernels, middle(): pl.pallas_call(middle_kernel, grid=(rows // BLOCK,), in_specs=[row, row,...  44.9 us
    pallas_call x1, Pallas kernels, outer_rest(): pl.pallas_call(outer_rest_kernel, grid=(6,), in_specs=[whole((rows, width...  22.1 us
    broadcast_in_dim x10, local copies, waits for them, and re-layouts, unpacked(): return [vector[None, :] for vector in vectors]  11.6 us
    unnamed x14, local copies, waits for them, and re-layouts  9.94 us

profile of v4, /device:TPU:0, one launch (start us, length us, event | category | flops | bytes accessed | tf_op | source)
XLA Modules:
  0.0 312.4 jit_solution(1517310201905674173)
XLA Ops:
  0.7 0.7 copy-done
  2.1 1.3 broadcast_in_dim.76.gain_ref
  3.4 1.3 broadcast_in_dim.77.shift_ref
  4.6 0.7 broadcast_in_dim.78
  5.3 0.7 broadcast_in_dim.80
  6.0 1.3 broadcast_in_dim.85.sg_ref
  7.3 1.3 broadcast_in_dim.86.ss_ref
  8.5 1.3 broadcast_in_dim.87.ob_ref
  9.8 1.3 broadcast_in_dim.88.fg_ref
  11.1 1.3 broadcast_in_dim.89.fs_ref
  12.4 1.3 broadcast_in_dim.93.db_ref
  13.7 1.2 compare_select_fusion.start_ref
  15.6 1.5 fusion.alive_ref
  17.1 3.7 %constant_dynamic-slice_fusion = (bf16[1024,768]{1,0:T(8,128)(2,1)}, bf16[1024,768]{1,0:T(8,128)(2,1)}) fusion(bf16[2048,768]{1,0:T(8,128)(2,1)} %param.19, s32[]{:T(128)S(6)} %select_n.26, bf16[2048,768]{1,0:T(8,128)(2,1)} %param.18), kind=kLoop, calls=%fused_computation.9 | loop fusion | bytes 6291460 | tf_op jit(solution)/shard_map/dynamic_slice | solution.py:1040
  20.8 96.7 %front.1 = (bf16[1024,2304]{1,0:T(8,128)(2,1)}, bf16[1024,768]{1,0:T(8,128)(2,1)}, f32[1024,768]{1,0:T(8,128)}, f32[6,2,1024]{2,1,0:T(2,128)}, bf16[6,2,2,2,2,48...) custom-call(bf16[1024,768]{1,0:T(8,128)(2,1)} %get-tuple-element.77.x_ref, ...), custom_call_target="tpu_custom_call" | custom-call | tf_op jit(solution)/shard_map/front/pallas_call | solution.py:616
  117.6 44.9 %middle.1 = (f32[1024,768]{1,0:T(8,128)}, bf16[1024,768]{1,0:T(8,128)(2,1)}, bf16[1024,768]{1,0:T(8,128)(2,1)}, bf16[1024,768]{1,0:T(8,128)(2,1)}, bf16[1024,768...) custom-call(bf16[1024,768]{1,0:T(8,128)(2,1)} %get-tuple-element.77., ...), custom_call_target="tpu_custom_call" | custom-call | tf_op jit(solution)/shard_map/middle/pallas_call | solution.py:319
  162.4 22.1 %outer_rest.1 = bf16[6,768,1152]{2,1,0:T(8,128)(2,1)} custom-call(bf16[1024,768]{1,0:T(8,128)(2,1)} %get-tuple-element.50.nffn_ref, bf16[1024,3072]{1,0:T(8,128)(2,1)} %get-tuple-element.51.gup_ref, bf16[1024,768]{1,0:T(8,128)(2,1)} %get-tuple-element.52.mixed_ref, bf16[1024,768]{1,0:T(8,128)(2,1)} %get-tuple-element.53.gbranch_ref, ...), custom_call_target="tpu_custom_call" | custom-call | tf_op jit(solution)/shard_map/outer_rest/pallas_call | solution.py:664
  184.5 115.8 %back.1 = (f32[2,1024,768]{2,1,0:T(8,128)}, f32[2,1024,384]{2,1,0:T(8,128)}, f32[48,3072]{1,0:T(8,128)}, f32[96,768]{1,0:T(8,128)}, f32[16,128]{1,0:T(8,128)}, /*index=5*/f32[8,128]{1,0:T(8,128)}) custom-call(bf16[1024,2304]{1,0:T(8,128)(2,1)} %get-tuple-element.40.projected_ref, bf16[1024,768]{1,0:T(8,128)(2,1)} %get-tuple-element.43.gctx_ref, ...), custom_call_target="tpu_custom_call" | custom-call | tf_op jit(solution)/shard_map/back/pallas_call | solution.py:945
  300.3 1.3 slice_bitcast_fusion.1
  301.6 1.5 slice_bitcast_fusion
  303.1 6.1 %copy.39 = f32[2048,768]{1,0:T(8,128)} copy(f32[2048,768]{1,0:T(8,128)} %bitcast.40) | data formatting | bytes 12582912
  309.2 1.7 copy.40
  310.8 0.8 copy.41
  311.7 0.7 copy.42
  (16 shorter events, 1.5 us)
Async XLA Ops:
  0.7 0.7 copy-start
  303.1 6.1 %copy-start.2 = (f32[2,1024,384]{2,1,0:T(8,128)S(1)}, f32[2,1024,384]{2,1,0:T(8,128)}, u32[]{:S(2)}) copy-start(f32[2,1024,384]{2,1,0:T(8,128)} %get-tuple-element.58) | copy-start | bytes 9437188
  303.1 9.3 %copy-start.1 = (s32[2,8]{1,0:T(2,128)S(1)}, s32[2,8]{1,0:T(2,128)}, u32[]{:S(2)}) copy-start(s32[2,8]{1,0:T(2,128)} %param.20) | copy-start | bytes 196
  309.2 1.7 copy-start.3
  309.2 2.5 copy-start.4
